TPU v7x, 512 devices: a whole 4x4x16 slice. The times are simulated.
512 devices in a mesh: section: 4 (over x), dp: 16 (over z), expert: 8 (over y, core).
Axes of the slice: x: 4, y: 4, z: 16, core: 2. Of those that a mesh axis runs over, the one named last changes fastest.
Arguments:
- section_input: bfloat16 [4, 16384, 1024], P('section', ('dp', 'expert')), may hold values from -6 to 6
- saved_input: bfloat16 [4, 16384, 1024], P('section', ('dp', 'expert')), may hold values from -6 to 6
- cotangent: bfloat16 [4, 16384, 1024], P('section', ('dp', 'expert')), may hold values from -6 to 6
- routes_forward: int32 [4, 16384, 8], P('section', ('dp', 'expert')), may hold values from 0 to 63, as said below
- gates_forward: float32 [4, 16384, 8], P('section', ('dp', 'expert')), may hold values from 0.5 to 2
- routes_backward: int32 [4, 16384, 8], P('section', ('dp', 'expert')), may hold values from 0 to 63, as said below
- gates_backward: float32 [4, 16384, 8], P('section', ('dp', 'expert')), may hold values from 0.5 to 2
- gate_weight: bfloat16 [4, 8, 1024, 512], P('section', 'expert', 'dp'), may hold values from -0.1875 to 0.1875
- up_weight: bfloat16 [4, 8, 1024, 512], P('section', 'expert', 'dp'), may hold values from -0.1875 to 0.1875
- down_weight: bfloat16 [4, 8, 512, 1024], P('section', 'expert', 'dp'), may hold values from -0.25 to 0.25
Outputs:
- handed: bfloat16 [4, 16384, 1024], P('section', ('dp', 'expert'))
- grad_back: bfloat16 [4, 16384, 1024], P('section', ('dp', 'expert'))
- grad_gate: float32 [4, 8, 1024, 512], P('section', 'expert', 'dp')
- grad_up: float32 [4, 8, 1024, 512], P('section', 'expert', 'dp')
- grad_down: float32 [4, 8, 512, 1024], P('section', 'expert', 'dp')
Inputs may be any that keep to these rules, and one draw needn't show every extreme that they name: `routes_forward`: each token names 8 different experts. In every layer, every block of 128 tokens of one device names each expert below 8 between 1 and 32 times, and in every layer some expert below 8 is named exactly 32 times by every block. `routes_backward`: as routes_forward.
All inputs are finite; a program needn't handle non-finite values.
Results may differ from a plain program's by a relative error of at most 0.017.
Values may be sent and summed in bfloat16 or wider, within the bound.
No kernel may reach another device: no remote copies, remote signals or barrier semaphores. Data moves between devices by JAX's collectives and lax.ppermute only.
A program may use at most 64 MiB of HBM per device.

v0:
```python
import math

import jax
import jax.numpy as jnp
from jax import lax
from jax.sharding import PartitionSpec as P

TOPK = 8
CAP = 32


EPSILON = 1e-06


def from_behind(array, axis, by):
    size = lax.axis_size(axis)
    return lax.ppermute(array, axis, [(i, (i + by) % size) for i in range(size)])


def normalize(values):
    widened = values.astype(jnp.float32)
    factor = lax.rsqrt(jnp.mean(widened * widened, axis=-1, keepdims=True) + EPSILON)
    return (widened * factor, factor)


def slot_table(listed, window):
    hit_table = (listed[:, :, None] == jnp.arange(window, dtype=jnp.int32)[None, None, :]).astype(
        jnp.int32
    )
    flat_hits = hit_table.reshape(-1, window)
    before = jnp.cumsum(flat_hits, axis=0) - flat_hits
    ranked = jnp.sum(before * flat_hits, axis=1).reshape(listed.shape)
    return jnp.where(listed < window, listed * CAP + ranked, window * CAP)


def slot_owner(slot_ids, window):
    token_total = slot_ids.shape[0]
    token_index = jnp.repeat(jnp.arange(token_total, dtype=jnp.int32), slot_ids.shape[1])
    owners = (
        jnp.full((window * CAP + 1,), token_total, jnp.int32)
        .at[slot_ids.reshape(-1)]
        .set(token_index)
    )
    return owners[: window * CAP]


def slot_gates(slot_ids, gate_vals, window):
    filled = (
        jnp.zeros((window * CAP + 1,), jnp.float32)
        .at[slot_ids.reshape(-1)]
        .set(gate_vals.reshape(-1))
    )
    return filled[: window * CAP]


def pad_rows(row_table):
    extra = jnp.zeros((1, row_table.shape[-1]), row_table.dtype)
    return jnp.concatenate([row_table, extra], axis=0)


def local(
    section_input,
    saved_input,
    cotangent,
    routes_forward,
    gates_forward,
    routes_backward,
    gates_backward,
    gate_weight,
    up_weight,
    down_weight,
):
    window = lax.axis_size("expert")
    token_count = section_input.shape[1]
    model_width = section_input.shape[2]
    hidden_width = gate_weight.shape[3]
    gathered = (
        lax.all_gather(gate_weight, "dp", axis=2, tiled=True),
        lax.all_gather(up_weight, "dp", axis=2, tiled=True),
        lax.all_gather(down_weight, "dp", axis=2, tiled=True),
    )
    gate_full = gathered[0][0, 0]
    up_full = gathered[1][0, 0]
    down_full = gathered[2][0, 0]
    contract = (((1,), (1,)), ((), ()))
    normed, _ = normalize(section_input[0])
    slot_ids = slot_table(routes_forward[0], window)
    owners = slot_owner(slot_ids, window)
    sent_forward = pad_rows(normed.astype(jnp.bfloat16))[owners].reshape(window, CAP, model_width)
    saved_float, saved_scale = normalize(saved_input[0])
    back_slots = slot_table(routes_backward[0], window)
    back_owners = slot_owner(back_slots, window)
    back_gates = slot_gates(back_slots, gates_backward[0], window)
    sent_backward = pad_rows(saved_float.astype(jnp.bfloat16))[back_owners].reshape(
        window, CAP, model_width
    )
    grad_sent = (
        back_gates[:, None] * pad_rows(cotangent[0])[back_owners].astype(jnp.float32)
    ).astype(jnp.bfloat16)
    grad_sent = grad_sent.reshape(window, CAP, model_width)
    received = lax.all_to_all(sent_forward, "expert", split_axis=0, concat_axis=0, tiled=True)
    flat_rows = received.reshape(-1, model_width)
    gate_act = jnp.dot(flat_rows, gate_full, preferred_element_type=jnp.float32)
    up_act = jnp.dot(flat_rows, up_full, preferred_element_type=jnp.float32)
    hidden = (gate_act * jax.nn.sigmoid(gate_act) * up_act).astype(jnp.bfloat16)
    produced = jnp.dot(hidden, down_full, preferred_element_type=jnp.float32).astype(jnp.bfloat16)
    returned = lax.all_to_all(
        produced.reshape(received.shape), "expert", split_axis=0, concat_axis=0, tiled=True
    )
    received = (
        lax.all_to_all(sent_backward, "expert", split_axis=0, concat_axis=0, tiled=True),
        lax.all_to_all(grad_sent, "expert", split_axis=0, concat_axis=0, tiled=True),
    )
    received_rows = received[0]
    lead = received_rows.shape[:2]
    flat_rows = received_rows.reshape(-1, model_width)
    flat_grads = received[1].reshape(-1, model_width)
    gate_act = jnp.dot(flat_rows, gate_full, preferred_element_type=jnp.float32)
    up_act = jnp.dot(flat_rows, up_full, preferred_element_type=jnp.float32)
    sigma = jax.nn.sigmoid(gate_act)
    activated = gate_act * sigma
    hidden = (activated * up_act).astype(jnp.bfloat16)
    grad_hidden = lax.dot_general(
        flat_grads, down_full, contract, preferred_element_type=jnp.float32
    )
    grad_gate = (grad_hidden * up_act * sigma * (1.0 + gate_act * (1.0 - sigma))).astype(
        jnp.bfloat16
    )
    grad_up = (grad_hidden * activated).astype(jnp.bfloat16)
    grad_input = lax.dot_general(grad_gate, gate_full, contract, preferred_element_type=jnp.float32)
    grad_input = grad_input + lax.dot_general(
        grad_up, up_full, contract, preferred_element_type=jnp.float32
    )
    hidden, grad_gate, grad_up, grad_input = (
        hidden.reshape(lead + (hidden_width,)),
        grad_gate.reshape(lead + (hidden_width,)),
        grad_up.reshape(lead + (hidden_width,)),
        grad_input.astype(jnp.bfloat16).reshape(lead + (model_width,)),
    )
    sent_home = lax.all_to_all(grad_input, "expert", split_axis=0, concat_axis=0, tiled=True)
    grad_returned, expert_rows, expert_grads, hidden, grad_gate, grad_up = (
        sent_home,
        received[0],
        received[1],
        hidden,
        grad_gate,
        grad_up,
    )
    returned_pad = pad_rows(returned.reshape(window * CAP, model_width))
    mixed_sum = section_input[0].astype(jnp.float32)
    for slot_pos in range(TOPK):
        mixed_sum = mixed_sum + gates_forward[0][:, slot_pos, None] * returned_pad[
            slot_ids[:, slot_pos]
        ].astype(jnp.float32)
    handed = from_behind(mixed_sum.astype(jnp.bfloat16)[None], "section", 1)
    grad_pad = pad_rows(grad_returned.reshape(window * CAP, model_width))
    token_grad = jnp.zeros((token_count, model_width), jnp.float32)
    for slot_pos in range(TOPK):
        token_grad = token_grad + grad_pad[back_slots[:, slot_pos]].astype(jnp.float32)
    mean_term = jnp.mean(saved_float * token_grad, axis=-1, keepdims=True)
    input_grad = cotangent[0].astype(jnp.float32) + saved_scale * (
        token_grad - saved_float * mean_term
    )
    grad_back = from_behind(input_grad.astype(jnp.bfloat16)[None], "section", -1)
    rows_flat = expert_rows.reshape(-1, model_width)
    grads_flat = expert_grads.reshape(-1, model_width)
    hidden_flat = hidden.reshape(-1, hidden_width)
    gate_up = jnp.concatenate(
        [grad_gate.reshape(-1, hidden_width), grad_up.reshape(-1, hidden_width)], axis=1
    )
    transposed = (((0,), (0,)), ((), ()))
    left_part = rows_flat
    summed_in = lax.psum_scatter(
        lax.dot_general(left_part, gate_up, transposed, preferred_element_type=jnp.float32).astype(
            jnp.bfloat16
        ),
        "dp",
        scatter_dimension=0,
        tiled=True,
    ).astype(jnp.float32)
    left_part = hidden_flat
    summed_out = lax.psum_scatter(
        lax.dot_general(
            left_part, grads_flat, transposed, preferred_element_type=jnp.float32
        ).astype(jnp.bfloat16),
        "dp",
        scatter_dimension=0,
        tiled=True,
    ).astype(jnp.float32)
    grad_scale = 1.0 / math.sqrt(lax.axis_size("dp") * token_count)
    grad_gate_out = (summed_in[:, :hidden_width] * grad_scale)[None, None]
    grad_up_out = (summed_in[:, hidden_width:] * grad_scale)[None, None]
    grad_down_out = (summed_out * grad_scale)[None, None]
    return (handed, grad_back, grad_gate_out, grad_up_out, grad_down_out)


def solution(mesh):
    return jax.shard_map(
        local,
        mesh=mesh,
        in_specs=(
            P("section", ("dp", "expert"), None),
            P("section", ("dp", "expert"), None),
            P("section", ("dp", "expert"), None),
            P("section", ("dp", "expert"), None),
            P("section", ("dp", "expert"), None),
            P("section", ("dp", "expert"), None),
            P("section", ("dp", "expert"), None),
            P("section", "expert", "dp", None),
            P("section", "expert", "dp", None),
            P("section", "expert", "dp", None),
        ),
        out_specs=(
            P("section", ("dp", "expert"), None),
            P("section", ("dp", "expert"), None),
            P("section", "expert", "dp", None),
            P("section", "expert", "dp", None),
            P("section", "expert", "dp", None),
        ),
        check_vma=False,
    )
```

profile of v0, /device:TPU:6, one launch (start us, length us, event | category | flops | bytes accessed | tf_op | source)
XLA Modules:
  0.0 379.7 jit_solution(1343728989343063745)
XLA Ops:
  7.2 0.7 all-gather.4.cloned.1.call-update
  7.9 0.7 all-gather.6.cloned.1.call-update
  8.7 0.7 all-gather.8.cloned.1.call-update
  9.4 0.8 copy.28
  10.5 1.1 fusion.34
  11.6 1.1 fusion.22
  12.7 2.3 reduce-window.16
  15.9 4.3 %scatter_custom_fusion.2 = s32[257]{0:T(512)S(1)} fusion(s32[1024]{0:T(1024)S(1)} %bitcast.187, s32[1024]{0:T(1024)S(1)} %reshape.855, s32[]{:T(128)} %constant.17.clone.1), kind=kCustom, calls=%fused_computation.181 | custom fusion | bytes 1032 | tf_op jit(solution)/shard_map/scatter | solution.py:42
  20.2 2.0 gather_fusion.10
  22.2 4.5 %all-to-all-start.3 = ((bf16[8,32,1024]{2,1,0:T(8,128)(2,1)}), bf16[8,32,1024]{2,1,0:T(8,128)(2,1)S(1)}, u32[]{:S(2)}, u32[]{:S(2)}) async-start(bf16[8,32,1024]{2,1,0:T(8,128)(2,1)} %bitcast.37), calls=%async_computation.3 | async-start | bytes 1048576 | tf_op jit(solution)/shard_map/all_to_all | solution.py:111
  26.9 2.3 reduce-window.14
  29.7 1.2 gather_fusion.9
  31.1 4.3 %scatter_custom_fusion.1 = f32[257]{0:T(512)S(1)} fusion(s32[1024]{0:T(1024)S(1)} %bitcast.188, f32[1024]{0:T(1024)S(1)} %reshape.847, f32[]{:T(128)} %constant.13.clone.1), kind=kCustom, calls=%fused_computation.179 | custom fusion | bytes 1032 | tf_op jit(solution)/shard_map/scatter | solution.py:51
  35.6 1.0 fusion.2
  37.0 4.4 %all-to-all-start.2 = ((bf16[8,32,1024]{2,1,0:T(8,128)(2,1)}), bf16[8,32,1024]{2,1,0:T(8,128)(2,1)S(1)}, u32[]{:S(2)}, u32[]{:S(2)}) async-start(bf16[8,32,1024]{2,1,0:T(8,128)(2,1)} %fusion.2), calls=%async_computation.2 | async-start | bytes 1048576 | tf_op jit(solution)/shard_map/all_to_all | solution.py:112
  41.4 43.8 %all-gather.4.cloned.1.call-done = bf16[1,1,1024,512]{3,2,1,0:T(8,128)(2,1)} async-done(((bf16[1,1,64,512]{3,2,1,0:T(8,128)(2,1)}), bf16[1,1,1024,512]{3,2,1,0:T(8,128)(2,1)}) %all-gather.4.cloned.1.call-update) | async-done | bytes 1048592 | tf_op jit(solution)/shard_map/all_gather | solution.py:78
  85.2 1.7 fusion.13
  86.8 68.0 %all-gather.6.cloned.1.call-done = bf16[1,1,1024,512]{3,2,1,0:T(8,128)(2,1)} async-done(((bf16[1,1,64,512]{3,2,1,0:T(8,128)(2,1)}), bf16[1,1,1024,512]{3,2,1,0:T(8,128)(2,1)}) %all-gather.6.cloned.1.call-update) | async-done | bytes 1048592 | tf_op jit(solution)/shard_map/all_gather | solution.py:79
  154.9 1.7 fusion.7
  156.6 1.5 convolution_convert_fusion.1
  158.5 4.3 %scatter_custom_fusion = s32[257]{0:T(512)S(1)} fusion(s32[1024]{0:T(1024)S(1)} %bitcast.189, s32[1024]{0:T(1024)S(1)} %reshape.855, s32[]{:T(128)} %constant.17.clone.1), kind=kCustom, calls=%fused_computation.183 | custom fusion | bytes 1032 | tf_op jit(solution)/shard_map/scatter | solution.py:42
  163.1 61.5 %all-gather.8.cloned.1.call-done = bf16[1,1,512,1024]{3,2,1,0:T(8,128)(2,1)} async-done(((bf16[1,1,32,1024]{3,2,1,0:T(8,128)(2,1)}), bf16[1,1,512,1024]{3,2,1,0:T(8,128)(2,1)}) %all-gather.8.cloned.1.call-update) | async-done | bytes 1048592 | tf_op jit(solution)/shard_map/all_gather | solution.py:80
  224.7 1.9 multiply_convert_fusion.1
  226.6 2.1 convolution_convert_fusion
  228.8 2.0 gather_fusion
  230.7 4.4 %all-to-all-start = ((bf16[8,32,1024]{2,1,0:T(8,128)(2,1)}), bf16[8,32,1024]{2,1,0:T(8,128)(2,1)S(1)}, u32[]{:S(2)}, u32[]{:S(2)}) async-start(bf16[8,32,1024]{2,1,0:T(8,128)(2,1)} %bitcast.6), calls=%async_computation | async-start | bytes 1048576 | tf_op jit(solution)/shard_map/all_to_all | solution.py:101
  235.5 0.6 pad_clamp_fusion.9
  236.7 0.6 pad_clamp_fusion.13
  237.7 0.6 pad_clamp_fusion.15
  238.3 1.6 slice_bitcast_fusion.7
  239.9 5.5 %all-to-all-done = bf16[8,32,1024]{2,1,0:T(8,128)(2,1)S(1)} async-done(((bf16[8,32,1024]{2,1,0:T(8,128)(2,1)}), bf16[8,32,1024]{2,1,0:T(8,128)(2,1)S(1)}, u32[]{:S(2)}, u32[]{:S(2)}) %all-to-all-start) | async-done | bytes 524320 | tf_op jit(solution)/shard_map/all_to_all | solution.py:101
  245.5 1.2 fusion.15
  246.7 3.0 convolution_convert_fusion.2
  249.7 3.7 all-to-all-start.1
  253.9 1.3 fusion
  255.1 8.3 %all-to-all-done.1 = bf16[8,32,1024]{2,1,0:T(8,128)(2,1)S(1)} async-done(((bf16[8,32,1024]{2,1,0:T(8,128)(2,1)}), bf16[8,32,1024]{2,1,0:T(8,128)(2,1)S(1)}, u32[]{:S(2)}, u32[]{:S(2)}) %all-to-all-start.1) | async-done | bytes 524320 | tf_op jit(solution)/shard_map/all_to_all | solution.py:107
  263.5 3.5 all-to-all-start.4
  267.0 0.6 pad_clamp_fusion.4
  268.2 1.0 gather_fusion.8
  269.2 1.0 gather_fusion.7
  270.2 1.0 gather_fusion.6
  271.2 1.0 gather_fusion.5
  272.1 1.0 gather_fusion.4
  273.1 1.0 gather_fusion.3
  274.2 1.0 gather_fusion.2
  275.2 1.0 gather_fusion.1
  276.2 1.2 fusion.33
  277.4 2.5 collective-permute-start
  280.0 0.9 gather_fusion.18
  280.8 0.9 gather_fusion.17
  281.7 0.9 gather_fusion.16
  282.5 0.9 gather_fusion.15
  283.4 1.0 gather_fusion.14
  284.4 1.0 gather_fusion.13
  285.4 1.1 gather_fusion.12
  286.5 1.1 gather_fusion.11
  288.3 3.4 collective-permute-start.1
  291.7 8.0 %collective-permute-done.1 = bf16[1,128,1024]{2,1,0:T(8,128)(2,1)S(1)} collective-permute-done((bf16[1,128,1024]{2,1,0:T(8,128)(2,1)S(1)}, bf16[1,128,1024]{2,1,0:T(8,128)(2,1)S(1)}, u32[]{:S(2)}, u32[]{:S(2)}) %collective-permute-start.1) | collective-permute-done | bytes 262176 | tf_op jit(solution)/shard_map/ppermute | solution.py:17
  299.8 1.5 multiply_bitcast_fusion
  301.3 68.9 %reduce-scatter.3.cloned.1.call-done = bf16[64,1024]{1,0:T(8,128)(2,1)} async-done(((bf16[1024,1024]{1,0:T(8,128)(2,1)}), bf16[64,1024]{1,0:T(8,128)(2,1)}) %reduce-scatter.3.cloned.1.call-update) | async-done | bytes 131088 | tf_op jit(solution)/shard_map/reduce_scatter | solution.py:173
  370.1 0.9 convert_element_type.358
  371.1 0.7 fusion.50
  371.8 0.7 copy.39
  372.5 0.7 copy.40
  (106 shorter events, 6.8 us)
Async XLA Ops:
  7.2 78.0 %all-gather.4.cloned.1.call-start = ((), (), s32[]{:S(2)}) async-start(), calls=%async_computation.7 | async-start | bytes 1114112 | tf_op jit(solution)/shard_map/all_gather | solution.py:78
  7.9 147.0 %all-gather.6.cloned.1.call-start = ((), (), s32[]{:S(2)}) async-start(), calls=%async_computation.8 | async-start | bytes 1114112 | tf_op jit(solution)/shard_map/all_gather | solution.py:79
  8.6 216.0 %all-gather.8.cloned.1.call-start = ((), (), s32[]{:S(2)}) async-start(), calls=%async_computation.9 | async-start | bytes 1114112 | tf_op jit(solution)/shard_map/all_gather | solution.py:80
  11.6 3.9 %copy-start.7 = (f32[128]{0:T(128)}, f32[128]{0:T(128)S(1)}, u32[]{:S(2)}) copy-start(f32[128]{0:T(128)S(1)} %add_rsqrt_fusion) | copy-start | bytes 1540
  20.2 6.5 %copy-start.9 = (s32[1,128,8]{1,2,0:T(8,128)S(1)}, s32[1,128,8]{1,2,0:T(8,128)}, u32[]{:S(2)}) copy-start(s32[1,128,8]{1,2,0:T(8,128)} %param.13) | copy-start | bytes 12292
  20.2 9.5 %copy-start.4 = (bf16[1,128,1024]{2,1,0:T(8,128)(2,1)S(1)}, bf16[1,128,1024]{2,1,0:T(8,128)(2,1)}, u32[]{:S(2)}) copy-start(bf16[1,128,1024]{2,1,0:T(8,128)(2,1)} %param.12) | copy-start | bytes 786436
  22.2 14.8 %all-to-all-start.3 = ((bf16[8,32,1024]{2,1,0:T(8,128)(2,1)}), bf16[8,32,1024]{2,1,0:T(8,128)(2,1)S(1)}, u32[]{:S(2)}, u32[]{:S(2)}) async-start(bf16[8,32,1024]{2,1,0:T(8,128)(2,1)} %bitcast.37), calls=%async_computation.3 | async-start | bytes 1048576 | tf_op jit(solution)/shard_map/all_to_all | solution.py:111
  29.7 1.2 copy-start.10
  37.0 119.6 %all-to-all-start.2 = ((bf16[8,32,1024]{2,1,0:T(8,128)(2,1)}), bf16[8,32,1024]{2,1,0:T(8,128)(2,1)S(1)}, u32[]{:S(2)}, u32[]{:S(2)}) async-start(bf16[8,32,1024]{2,1,0:T(8,128)(2,1)} %fusion.2), calls=%async_computation.2 | async-start | bytes 1048576 | tf_op jit(solution)/shard_map/all_to_all | solution.py:112
  41.3 258.4 %reduce-scatter.5.cloned.1.call-start = ((), (), s32[]{:S(2)}) async-start(), calls=%async_computation.11 | async-start | bytes 1114112 | tf_op jit(solution)/shard_map/reduce_scatter | solution.py:182
  156.5 6.5 %copy-start.6 = (f32[256,512]{1,0:T(8,128)}, f32[256,512]{1,0:T(8,128)S(1)}, u32[]{:S(2)}) copy-start(f32[256,512]{1,0:T(8,128)S(1)} %fusion.7) | copy-start | bytes 1572868
  156.5 6.3 %copy-start.3 = (bf16[1,128,1024]{2,1,0:T(8,128)(2,1)S(1)}, bf16[1,128,1024]{2,1,0:T(8,128)(2,1)}, u32[]{:S(2)}) copy-start(bf16[1,128,1024]{2,1,0:T(8,128)(2,1)} %param.10) | copy-start | bytes 786436
  158.1 212.0 %reduce-scatter.3.cloned.1.call-start = ((), (), s32[]{:S(2)}) async-start(), calls=%async_computation.10 | async-start | bytes 2228224 | tf_op jit(solution)/shard_map/reduce_scatter | solution.py:173
  230.7 14.7 %copy-start = (bf16[1,1,1024,512]{3,2,1,0:T(8,128)(2,1)S(1)}, bf16[1,1,1024,512]{3,2,1,0:T(8,128)(2,1)}, u32[]{:S(2)}) copy-start(bf16[1,1,1024,512]{3,2,1,0:T(8,128)(2,1)} %all-gather.4.cloned.1.call-done) | copy-start | bytes 3145732
  230.7 16.0 %copy-start.1 = (bf16[1,1,1024,512]{3,2,1,0:T(8,128)(2,1)S(1)}, bf16[1,1,1024,512]{3,2,1,0:T(8,128)(2,1)}, u32[]{:S(2)}) copy-start(bf16[1,1,1024,512]{3,2,1,0:T(8,128)(2,1)} %all-gather.6.cloned.1.call-done) | copy-start | bytes 3145732
  230.7 14.7 %all-to-all-start = ((bf16[8,32,1024]{2,1,0:T(8,128)(2,1)}), bf16[8,32,1024]{2,1,0:T(8,128)(2,1)S(1)}, u32[]{:S(2)}, u32[]{:S(2)}) async-start(bf16[8,32,1024]{2,1,0:T(8,128)(2,1)} %bitcast.6), calls=%async_computation | async-start | bytes 1048576 | tf_op jit(solution)/shard_map/all_to_all | solution.py:101
  249.7 13.7 %all-to-all-start.1 = ((bf16[8,32,1024]{2,1,0:T(8,128)(2,1)}), bf16[8,32,1024]{2,1,0:T(8,128)(2,1)S(1)}, u32[]{:S(2)}, u32[]{:S(2)}) async-start(bf16[8,32,1024]{2,1,0:T(8,128)(2,1)} %bitcast.181), calls=%async_computation.1 | async-start | bytes 1048576 | tf_op jit(solution)/shard_map/all_to_all | solution.py:107
  263.5 16.4 %all-to-all-start.4 = ((bf16[8,32,1024]{2,1,0:T(8,128)(2,1)}), bf16[8,32,1024]{2,1,0:T(8,128)(2,1)S(1)}, u32[]{:S(2)}, u32[]{:S(2)}) async-start(bf16[8,32,1024]{2,1,0:T(8,128)(2,1)} %bitcast.39), calls=%async_computation.4 | async-start | bytes 1048576 | tf_op jit(solution)/shard_map/all_to_all | solution.py:140
  274.1 2.0 copy-start.11
  274.1 2.0 copy-start.12
  274.1 2.0 copy-start.13
  274.1 2.0 copy-start.14
  274.1 2.0 copy-start.15
  274.2 2.0 copy-start.16
  274.2 2.0 copy-start.17
  274.2 2.0 copy-start.18
  277.4 14.3 %collective-permute-start = (bf16[1,128,1024]{2,1,0:T(8,128)(2,1)}, bf16[1,128,1024]{2,1,0:T(8,128)(2,1)S(1)}, u32[]{:S(2)}, u32[]{:S(2)}) collective-permute-start(bf16[1,128,1024]{2,1,0:T(8,128)(2,1)} %fusion.33), channel_id=1, source_target_pairs={{0,128},{128,256},{256,384},{384,0},{1,129},{129,257},{257,385},{3... | collective-permute-start | bytes 786440 | tf_op jit(solution)/shard_map/ppermute | solution.py:17
  285.4 2.3 copy-start.2
  285.4 2.3 copy-start.8
  286.5 1.6 copy-start.5
  288.3 11.4 %collective-permute-start.1 = (bf16[1,128,1024]{2,1,0:T(8,128)(2,1)S(1)}, bf16[1,128,1024]{2,1,0:T(8,128)(2,1)S(1)}, u32[]{:S(2)}, u32[]{:S(2)}) collective-permute-start(bf16[1,128,1024]{2,1,0:T(8,128)(2,1)S(1)} %fusion.39), channel_id=1, source_target_pairs={{0,384},{128,0},{256,128},{384,256},{1,385},{129,1},{257,129},{385... | collective-permute-start | bytes 786440 | tf_op jit(solution)/shard_map/ppermute | solution.py:17
Sparse Core Ops, SparseCore 0:
  10.1 75.0 all-gather.3
  87.3 67.5 all-gather.5
  157.0 67.6 all-gather.7
  227.3 68.3 reduce-scatter.4
  298.4 71.6 reduce-scatter.2
where the time goes:
time: 381 us; the launch traced here: 380 us
  waiting for transfers between devices  267 us (70%)
  local copies, waits for them, and re-layouts  39.5 us (10%)
  starting transfers between devices  26.4 us (7%)
  other arithmetic  17.9 us (5%)
  matrix products  14.8 us (4%)
  between operations  14.4 us (4%)
    reduce_scatter x1, waiting for transfers between devices, local(): lax.psum_scatter(lax.dot_general(left_part, gate_up, transposed, preferre...  68.9 us
    all_gather x1, waiting for transfers between devices, local(): lax.all_gather(up_weight, 'dp', axis=2, tiled=True)  68 us
    all_gather x1, waiting for transfers between devices, local(): lax.all_gather(down_weight, 'dp', axis=2, tiled=True)  61.5 us
    all_gather x1, waiting for transfers between devices, local(): lax.all_gather(gate_weight, 'dp', axis=2, tiled=True)  43.8 us
    scatter x2, local copies, waits for them, and re-layouts, slot_owner(): owners = jnp.full((window * CAP + 1,), token_total, jnp.int32).at[slot_id...  8.61 us
    all_to_all x1, waiting for transfers between devices, local(): lax.all_to_all(produced.reshape(received.shape), 'expert', split_axis=0,...  8.32 us
    ppermute x2, waiting for transfers between devices, from_behind(): lax.ppermute(array, axis, [(i, (i + by) % size) for i in range(size)])  8.05 us
    gather x8, local copies, waits for them, and re-layouts, local(): returned_pad[slot_ids[:, slot_pos]].astype(jnp.float32)  7.86 us
  transfers between devices with their start and end apart: 12, of which 8 were waited for; matrix products, arithmetic and copies ran while one was open for 18% of the time, Pallas kernels for 0%

commit v1 on v0

v1 whole, which is shorter than its diff:
```python
import math

import jax
import jax.numpy as jnp
from jax import lax
from jax.experimental import pallas as pl
from jax.experimental.pallas import tpu as pltpu
from jax.sharding import PartitionSpec as P

TOPK = 8
CAP = 32
EPSILON = 1e-06
F32 = jnp.float32
BF16 = jnp.bfloat16
CONTRACT_LAST = (((1,), (1,)), ((), ()))
CONTRACT_FIRST = (((0,), (0,)), ((), ()))
VMEM_LIMIT = 56 * 1024 * 1024


def from_behind(array, axis, by):
    size = lax.axis_size(axis)
    return lax.ppermute(array, axis, [(i, (i + by) % size) for i in range(size)])


def normalize(values):
    widened = values.astype(F32)
    factor = lax.rsqrt(jnp.mean(widened * widened, axis=-1, keepdims=True) + EPSILON)
    return (widened * factor, factor)


def slot_table(listed, window):
    hit_table = (listed[:, :, None] == jnp.arange(window, dtype=jnp.int32)[None, None, :]).astype(
        jnp.int32
    )
    flat_hits = hit_table.reshape(-1, window)
    before = jnp.cumsum(flat_hits, axis=0) - flat_hits
    ranked = jnp.sum(before * flat_hits, axis=1).reshape(listed.shape)
    return jnp.where(listed < window, listed * CAP + ranked, window * CAP)


def slot_owner(slot_ids, window):
    token_total = slot_ids.shape[0]
    token_index = jnp.repeat(jnp.arange(token_total, dtype=jnp.int32), slot_ids.shape[1])
    owners = (
        jnp.full((window * CAP + 1,), token_total, jnp.int32)
        .at[slot_ids.reshape(-1)]
        .set(token_index)
    )
    return owners[: window * CAP]


def slot_gates(slot_ids, gate_vals, window):
    filled = (
        jnp.zeros((window * CAP + 1,), F32).at[slot_ids.reshape(-1)].set(gate_vals.reshape(-1))
    )
    return filled[: window * CAP]


def pad_rows(row_table):
    extra = jnp.zeros((1, row_table.shape[-1]), row_table.dtype)
    return jnp.concatenate([row_table, extra], axis=0)


def dot(a, b):
    return jnp.dot(a, b, preferred_element_type=F32)


def weights_of(w_ref):
    parts, _, half = w_ref.shape
    rows = 2 * half // parts
    low = half // parts
    gate = w_ref[:, 0:rows, :].reshape(2 * half, half)
    up = w_ref[:, rows : 2 * rows, :].reshape(2 * half, half)
    down_a = w_ref[:, 2 * rows : 2 * rows + low, :].reshape(half, half)
    down_b = w_ref[:, 2 * rows + low : 3 * rows, :].reshape(half, half)
    return gate, up, down_a, down_b


def backward_body(w_ref, r_ref, p_ref, gg_ref, gu_ref):
    gate, up, down_a, down_b = weights_of(w_ref)
    parts, _, half = w_ref.shape
    rows = 2 * half // parts
    low = half // parts
    width = 2 * half
    saved = r_ref[:, CAP : 2 * CAP, :].reshape(-1, width)
    grads = r_ref[:, 2 * CAP : 3 * CAP, :].reshape(-1, width)
    gate_act = dot(saved, gate)
    up_act = dot(saved, up)
    sigma = jax.nn.sigmoid(gate_act)
    activated = gate_act * sigma
    hidden = (activated * up_act).astype(BF16)
    p_down_a = lax.dot_general(hidden, grads[:, :half], CONTRACT_FIRST, preferred_element_type=F32)
    p_ref[:, 2 * rows : 2 * rows + low, :] = p_down_a.astype(BF16).reshape(parts, low, half)
    p_down_b = lax.dot_general(hidden, grads[:, half:], CONTRACT_FIRST, preferred_element_type=F32)
    p_ref[:, 2 * rows + low : 3 * rows, :] = p_down_b.astype(BF16).reshape(parts, low, half)
    grad_hidden = lax.dot_general(
        grads[:, :half], down_a, CONTRACT_LAST, preferred_element_type=F32
    ) + lax.dot_general(grads[:, half:], down_b, CONTRACT_LAST, preferred_element_type=F32)
    grad_gate = (grad_hidden * up_act * sigma * (1.0 + gate_act * (1.0 - sigma))).astype(BF16)
    grad_up = (grad_hidden * activated).astype(BF16)
    gg_ref[...] = grad_gate
    gu_ref[...] = grad_up
    p_gate = lax.dot_general(saved, grad_gate, CONTRACT_FIRST, preferred_element_type=F32)
    p_ref[:, 0:rows, :] = p_gate.astype(BF16).reshape(parts, rows, half)
    p_up = lax.dot_general(saved, grad_up, CONTRACT_FIRST, preferred_element_type=F32)
    p_ref[:, rows : 2 * rows, :] = p_up.astype(BF16).reshape(parts, rows, half)


def forward_body(w_ref, r_ref, gg_ref, gu_ref, o_ref):
    gate, up, down_a, down_b = weights_of(w_ref)
    half = w_ref.shape[2]
    width = 2 * half
    window = r_ref.shape[0]
    fresh = r_ref[:, 0:CAP, :].reshape(-1, width)
    gate_act = dot(fresh, gate)
    up_act = dot(fresh, up)
    hidden = (gate_act * jax.nn.sigmoid(gate_act) * up_act).astype(BF16)
    o_ref[:, 0:CAP, :half] = dot(hidden, down_a).astype(BF16).reshape(window, CAP, half)
    o_ref[:, 0:CAP, half:] = dot(hidden, down_b).astype(BF16).reshape(window, CAP, half)
    grad_input = lax.dot_general(
        gg_ref[...], gate, CONTRACT_LAST, preferred_element_type=F32
    ) + lax.dot_general(gu_ref[...], up, CONTRACT_LAST, preferred_element_type=F32)
    o_ref[:, CAP : 2 * CAP, :] = grad_input.astype(BF16).reshape(window, CAP, width)


def expert_backward(gathered, received):
    half = gathered.shape[2]
    slots = received.shape[0] * CAP
    return pl.pallas_call(
        backward_body,
        out_shape=(
            jax.ShapeDtypeStruct(gathered.shape, BF16),
            jax.ShapeDtypeStruct((slots, half), BF16),
            jax.ShapeDtypeStruct((slots, half), BF16),
        ),
        compiler_params=pltpu.CompilerParams(vmem_limit_bytes=VMEM_LIMIT),
        cost_estimate=pl.CostEstimate(
            flops=2 * slots * half * half * 2 * 6,
            bytes_accessed=8 * 1024 * 1024,
            transcendentals=slots * half,
        ),
        name="expert_backward",
    )(gathered, received)


def expert_forward(gathered, received, grad_gate, grad_up):
    half = gathered.shape[2]
    window = received.shape[0]
    slots = window * CAP
    return pl.pallas_call(
        forward_body,
        out_shape=jax.ShapeDtypeStruct((window, 2 * CAP, 2 * half), BF16),
        compiler_params=pltpu.CompilerParams(vmem_limit_bytes=VMEM_LIMIT),
        cost_estimate=pl.CostEstimate(
            flops=2 * slots * half * half * 2 * 5,
            bytes_accessed=6 * 1024 * 1024,
            transcendentals=slots * half,
        ),
        name="expert_forward",
    )(gathered, received, grad_gate, grad_up)


def local(
    section_input,
    saved_input,
    cotangent,
    routes_forward,
    gates_forward,
    routes_backward,
    gates_backward,
    gate_weight,
    up_weight,
    down_weight,
):
    window = lax.axis_size("expert")
    parts = lax.axis_size("dp")
    token_count = section_input.shape[1]
    model_width = section_input.shape[2]
    half = gate_weight.shape[3]
    rows = gate_weight.shape[2]
    low = down_weight.shape[2]

    own = jnp.concatenate(
        [
            gate_weight[0, 0],
            up_weight[0, 0],
            down_weight[0, 0, :, :half],
            down_weight[0, 0, :, half:],
        ],
        axis=0,
    )
    gathered = lax.all_gather(own, "dp", axis=0, tiled=False)

    normed, _ = normalize(section_input[0])
    slot_ids = slot_table(routes_forward[0], window)
    owners = slot_owner(slot_ids, window)
    sent_forward = pad_rows(normed.astype(BF16))[owners].reshape(window, CAP, model_width)
    saved_float, saved_scale = normalize(saved_input[0])
    back_slots = slot_table(routes_backward[0], window)
    back_owners = slot_owner(back_slots, window)
    back_gates = slot_gates(back_slots, gates_backward[0], window)
    sent_backward = pad_rows(saved_float.astype(BF16))[back_owners].reshape(
        window, CAP, model_width
    )
    grad_sent = (back_gates[:, None] * pad_rows(cotangent[0])[back_owners].astype(F32)).astype(BF16)
    grad_sent = grad_sent.reshape(window, CAP, model_width)
    sent = jnp.concatenate([sent_forward, sent_backward, grad_sent], axis=1)
    received = lax.all_to_all(sent, "expert", split_axis=0, concat_axis=0, tiled=True)

    partial, grad_gate, grad_up = expert_backward(gathered, received)
    summed = lax.psum_scatter(
        partial.reshape(parts * 3 * rows, half), "dp", scatter_dimension=0, tiled=True
    )

    produced = expert_forward(gathered, received, grad_gate, grad_up)
    home = lax.all_to_all(produced, "expert", split_axis=0, concat_axis=0, tiled=True)

    returned_pad = pad_rows(home[:, :CAP].reshape(window * CAP, model_width))
    mixed_sum = section_input[0].astype(F32)
    for slot_pos in range(TOPK):
        mixed_sum = mixed_sum + gates_forward[0][:, slot_pos, None] * returned_pad[
            slot_ids[:, slot_pos]
        ].astype(F32)
    handed = from_behind(mixed_sum.astype(BF16)[None], "section", 1)
    grad_pad = pad_rows(home[:, CAP:].reshape(window * CAP, model_width))
    token_grad = jnp.zeros((token_count, model_width), F32)
    for slot_pos in range(TOPK):
        token_grad = token_grad + grad_pad[back_slots[:, slot_pos]].astype(F32)
    mean_term = jnp.mean(saved_float * token_grad, axis=-1, keepdims=True)
    input_grad = cotangent[0].astype(F32) + saved_scale * (token_grad - saved_float * mean_term)
    grad_back = from_behind(input_grad.astype(BF16)[None], "section", -1)

    grad_scale = 1.0 / math.sqrt(parts * token_count)
    scaled = summed.astype(F32) * grad_scale
    grad_gate_out = scaled[:rows][None, None]
    grad_up_out = scaled[rows : 2 * rows][None, None]
    grad_down_out = jnp.concatenate(
        [scaled[2 * rows : 2 * rows + low], scaled[2 * rows + low :]], axis=1
    )[None, None]
    return (handed, grad_back, grad_gate_out, grad_up_out, grad_down_out)


def solution(mesh):
    tokens = P("section", ("dp", "expert"), None)
    weights = P("section", "expert", "dp", None)
    return jax.shard_map(
        local,
        mesh=mesh,
        in_specs=(tokens,) * 7 + (weights,) * 3,
        out_specs=(tokens,) * 2 + (weights,) * 3,
        check_vma=False,
    )
```

time: 381 us -> 182 us (0.48)
  waiting for transfers between devices: 267 us -> 65.1 us
  blocking collectives: 0 us -> 26 us
  starting transfers between devices: 26.4 us -> 11.2 us
  matrix products: 14.8 us -> 0 us
  Pallas kernels: 0 us -> 11.4 us
  other arithmetic: 17.9 us -> 13.1 us
    all_gather x3 -> x1, waiting for transfers between devices: 173 us -> 26.3 us  [local(): gathered = lax.all_gather(own, 'dp', axis=0, tiled=False)]
    reduce_scatter x2 -> x1, waiting for transfers between devices: 68.9 us -> 18.3 us  [local(): lax.psum_scatter(partial.reshape(parts * 3 * rows, half), 'dp', scatter_d...]
    all_to_all x0 -> x1, blocking collectives: none -> 26 us  [local(): lax.all_to_all(sent, 'expert', split_axis=0, concat_axis=0, tiled=True)]
    all_to_all x5 -> x1, starting transfers between devices: 20.4 us -> 4.1 us  [local(): lax.all_to_all(produced, 'expert', split_axis=0, concat_axis=0, tiled=True)]
    dot_general x9 -> x0, matrix products: 14.8 us -> none  [the longest x1 2.99 us: local(): jnp.dot(hidden, down_full, preferred_element_type=jnp.float32)]
    pallas_call x0 -> x2, Pallas kernels: none -> 11.4 us  [the longest x1 6.27 us: expert_backward(): pl.pallas_call(backward_body, out_shape=(jax.ShapeDtypeStruct(gathered.sh...]
    all_to_all x5 -> x1, waiting for transfers between devices: 14.3 us -> 15.5 us  [local(): lax.all_to_all(produced, 'expert', split_axis=0, concat_axis=0, tiled=True)]
  transfers between devices with their start and end apart: 12 -> 5, of which waited for: 8 -> 4; matrix products, arithmetic and copies ran while one was open for 18% -> 26% of each run, Pallas kernels for 0% -> 3%
where the time goes in v1:
time: 182 us; the launch traced here: 181 us
  waiting for transfers between devices  65.1 us (36%)
  local copies, waits for them, and re-layouts  39.9 us (22%)
  blocking collectives  26 us (14%)
  between operations  14.5 us (8%)
  other arithmetic  13.1 us (7%)
  Pallas kernels  11.4 us (6%)
  starting transfers between devices  11.2 us (6%)
    all_gather x1, waiting for transfers between devices, local(): gathered = lax.all_gather(own, 'dp', axis=0, tiled=False)  26.3 us
    all_to_all x1, blocking collectives, local(): lax.all_to_all(sent, 'expert', split_axis=0, concat_axis=0, tiled=True)  26 us
    reduce_scatter x1, waiting for transfers between devices, local(): lax.psum_scatter(partial.reshape(parts * 3 * rows, half), 'dp', scatter_d...  18.3 us
    all_to_all x1, waiting for transfers between devices, local(): lax.all_to_all(produced, 'expert', split_axis=0, concat_axis=0, tiled=True)  15.5 us
    scatter x2, local copies, waits for them, and re-layouts, slot_owner(): owners = jnp.full((window * CAP + 1,), token_total, jnp.int32).at[slot_id...  8.61 us
    gather x8, local copies, waits for them, and re-layouts, local(): token_grad = token_grad + grad_pad[back_slots[:, slot_pos]].astype(F32)  8.29 us
    ppermute x2, starting transfers between devices, from_behind(): lax.ppermute(array, axis, [(i, (i + by) % size) for i in range(size)])  7.05 us
    gather x8, local copies, waits for them, and re-layouts, local(): returned_pad[slot_ids[:, slot_pos]].astype(F32)  6.89 us
  transfers between devices with their start and end apart: 5, of which 4 were waited for; matrix products, arithmetic and copies ran while one was open for 26% of the time, Pallas kernels for 3%

profile of v1, /device:TPU:6, one launch (start us, length us, event | category | flops | bytes accessed | tf_op | source)
XLA Modules:
  0.0 181.2 jit_solution(2368206945982202251)
XLA Ops:
  7.2 0.8 slice_bitcast_fusion.3
  8.0 1.6 pad_maximum_fusion.1
  9.7 0.8 copy.28
  10.6 2.3 %reduce-window.16 = s32[8,8,128]{2,1,0:T(8,128)S(1)} reduce-window(s32[8,8,128]{2,1,0:T(8,128)S(1)} %fusion.49, s32[]{:T(128)} %constant.9.clone.1), window={size=1x1x128 pad=0_0x0_0x127_0}, to_apply=%region_6.7 | reduce-window | flops 1040384 | bytes 65540 | tf_op jit(solution)/shard_map/reduce-window.2
  12.8 0.3 slice_reduce_fusion
  13.1 0.2 reduce-window.19
  13.5 0.8 copy.24
  14.6 0.1 lt.131
  14.7 0.1 mul.251
  14.9 0.8 copy.32
  15.8 4.3 %scatter_custom_fusion.2 = f32[257]{0:T(512)S(1)} fusion(s32[1024]{0:T(1024)S(1)} %bitcast.158, f32[1024]{0:T(1024)S(1)} %reshape.837, f32[]{:T(128)} %constant.12.clone.1), kind=kCustom, calls=%fused_computation.148 | custom fusion | bytes 1032 | tf_op jit(solution)/shard_map/scatter | solution.py:54
  20.2 1.0 concatenate.27
  21.2 1.1 fusion.18
  22.3 0.1 fusion.6
  22.4 4.3 %scatter_custom_fusion.1 = s32[257]{0:T(512)S(1)} fusion(s32[1024]{0:T(1024)S(1)} %bitcast.159, s32[1024]{0:T(1024)S(1)} %reshape.829, s32[]{:T(128)} %constant.16.clone.1), kind=kCustom, calls=%fused_computation.150 | custom fusion | bytes 1032 | tf_op jit(solution)/shard_map/scatter | solution.py:47
  26.8 1.2 gather_fusion.2
  27.9 1.2 gather_fusion.1
  29.1 2.3 %reduce-window.14 = s32[8,8,128]{2,1,0:T(8,128)S(1)} reduce-window(s32[8,8,128]{2,1,0:T(8,128)S(1)} %fusion.48, s32[]{:T(128)} %constant.9.clone.1), window={size=1x1x128 pad=0_0x0_0x127_0}, to_apply=%region_1.0 | reduce-window | flops 1040384 | bytes 65540 | tf_op jit(solution)/shard_map/reduce-window
  31.4 0.3 slice_reduce_fusion.1
  31.7 0.2 reduce-window.15
  32.1 0.1 lt.127
  32.2 0.1 mul.245
  32.3 4.3 %scatter_custom_fusion = s32[257]{0:T(512)S(1)} fusion(s32[1024]{0:T(1024)S(1)} %bitcast.160, s32[1024]{0:T(1024)S(1)} %reshape.829, s32[]{:T(128)} %constant.16.clone.1), kind=kCustom, calls=%fused_computation.152 | custom fusion | bytes 1032 | tf_op jit(solution)/shard_map/scatter | solution.py:47
  36.6 0.1 fusion.8
  36.8 0.1 fusion.9
  36.9 1.2 gather_fusion
  38.1 0.2 fusion
  38.3 0.1 pad_maximum_fusion
  38.4 26.0 %all_to_all.10.r_ref = bf16[8,96,1024]{2,1,0:T(8,128)(2,1)} all-to-all(bf16[8,96,1024]{2,1,0:T(8,128)(2,1)S(1)} %pad_maximum_fusion), channel_id=1, replica_groups=mesh['section'=4,'dp'=16,'expert'=8] {'expert'}, dimensions={0} | all-to-all | bytes 3145728 | tf_op jit(solution)/shard_map/all_to_all | solution.py:208
  64.4 26.3 %all-gather.3.cloned.1.call-done = bf16[3072,512]{1,0:T(8,128)(2,1)} async-done(((bf16[192,512]{1,0:T(8,128)(2,1)}), bf16[3072,512]{1,0:T(8,128)(2,1)}) %all-gather.3.cloned.1.call-update) | async-done | bytes 3145744 | tf_op jit(solution)/shard_map/all_gather | solution.py:192
  90.7 6.3 %expert_backward.1 = (bf16[16,192,512]{2,1,0:T(8,128)(2,1)}, bf16[256,512]{1,0:T(8,128)(2,1)}, bf16[256,512]{1,0:T(8,128)(2,1)}) custom-call(bf16[16,192,512]{2,1,0:T(8,128)(2,1)} %bitcast.143, bf16[8,96,1024]{2,1,0:T(8,128)(2,1)} %all_to_all.10.r_ref), custom_call_target="tpu_custom_call" | custom-call | flops 1610612736 | bytes 8388608 | tf_op jit(solution)/shard_map/expert_backward/pallas_call | solution.py:129
  97.0 0.4 fusion.32
  97.4 5.1 %expert_forward.1 = bf16[8,64,1024]{2,1,0:T(8,128)(2,1)} custom-call(bf16[16,192,512]{2,1,0:T(8,128)(2,1)} %bitcast.144, bf16[8,96,1024]{2,1,0:T(8,128)(2,1)} %all_to_all.10.r_ref, bf16[256,512]{1,0:T(8,128)(2,1)} %get-tuple-element.8.gg_ref, bf16[256,512]{1,0:T(8,128)(2,1)} %get-tuple-element.9.gu_ref), custom_call_target="tpu_custom_call" | custom-call | flops 1342177280 | bytes 6291456 | tf_op jit(solution)/shard_map/expert_forward/pallas_call | solution.py:150
  102.5 4.1 %all-to-all-start.1 = ((bf16[8,64,1024]{2,1,0:T(8,128)(2,1)}), bf16[8,64,1024]{2,1,0:T(8,128)(2,1)S(1)}, u32[]{:S(2)}, u32[]{:S(2)}) async-start(bf16[8,64,1024]{2,1,0:T(8,128)(2,1)} %expert_forward.1), calls=%async_computation.1 | async-start | bytes 2097152 | tf_op jit(solution)/shard_map/all_to_all | solution.py:216
  106.6 0.4 fusion.24
  107.1 15.5 %all-to-all-done.1 = bf16[8,64,1024]{2,1,0:T(8,128)(2,1)S(1)} async-done(((bf16[8,64,1024]{2,1,0:T(8,128)(2,1)}), bf16[8,64,1024]{2,1,0:T(8,128)(2,1)S(1)}, u32[]{:S(2)}, u32[]{:S(2)}) %all-to-all-start.1) | async-done | bytes 1048608 | tf_op jit(solution)/shard_map/all_to_all | solution.py:216
  122.7 0.9 gather_fusion.11
  123.6 0.9 gather_fusion.12
  124.4 0.9 gather_fusion.13
  125.3 0.9 gather_fusion.14
  126.1 0.9 gather_fusion.15
  127.0 0.9 gather_fusion.16
  127.9 1.6 gather_fusion.17
  129.4 1.6 gather_fusion.18
  131.0 1.4 fusion.7
  132.5 0.2 fusion.23
  132.7 2.7 %collective-permute-start.1 = (bf16[1,128,1024]{2,1,0:T(8,128)(2,1)S(1)}, bf16[1,128,1024]{2,1,0:T(8,128)(2,1)S(1)}, u32[]{:S(2)}, u32[]{:S(2)}) collective-permute-start(bf16[1,128,1024]{2,1,0:T(8,128)(2,1)S(1)} %fusion.23), channel_id=1, source_target_pairs={{0,384},{128,0},{256,128},{384,256},{1,385},{129,1},{257,129},{385... | collective-permute-start | bytes 786440 | tf_op jit(solution)/shard_map/ppermute | solution.py:22
  135.5 0.9 gather_fusion.3
  136.4 0.9 gather_fusion.4
  137.2 0.9 gather_fusion.5
  138.1 0.9 gather_fusion.6
  138.9 0.9 gather_fusion.7
  139.8 0.9 gather_fusion.8
  140.7 0.9 gather_fusion.9
  141.5 0.9 gather_fusion.10
  142.4 0.5 fusion.17
  142.9 4.3 %collective-permute-start = (bf16[1,128,1024]{2,1,0:T(8,128)(2,1)S(1)}, bf16[1,128,1024]{2,1,0:T(8,128)(2,1)S(1)}, u32[]{:S(2)}, u32[]{:S(2)}) collective-permute-start(bf16[1,128,1024]{2,1,0:T(8,128)(2,1)S(1)} %fusion.17), channel_id=1, source_target_pairs={{0,128},{128,256},{256,384},{384,0},{1,129},{129,257},{257,385},{3... | collective-permute-start | bytes 786440 | tf_op jit(solution)/shard_map/ppermute | solution.py:22
  147.2 5.0 %collective-permute-done = bf16[1,128,1024]{2,1,0:T(8,128)(2,1)S(1)} collective-permute-done((bf16[1,128,1024]{2,1,0:T(8,128)(2,1)S(1)}, bf16[1,128,1024]{2,1,0:T(8,128)(2,1)S(1)}, u32[]{:S(2)}, u32[]{:S(2)}) %collective-permute-start) | collective-permute-done | bytes 262176 | tf_op jit(solution)/shard_map/ppermute | solution.py:22
  152.3 18.3 %reduce-scatter.2.cloned.1.call-done = bf16[192,512]{1,0:T(8,128)(2,1)} async-done(((bf16[3072,512]{1,0:T(8,128)(2,1)}), bf16[192,512]{1,0:T(8,128)(2,1)}) %reduce-scatter.2.cloned.1.call-update) | async-done | bytes 196624 | tf_op jit(solution)/shard_map/reduce_scatter | solution.py:211
  170.6 1.0 convert_multiply_fusion.10
  171.6 0.7 slice_bitcast_fusion
  172.3 0.7 maximum_bitcast_fusion
  172.9 0.7 copy.39
  173.6 0.7 copy.40
  (58 shorter events, 1.6 us)
Async XLA Ops:
  7.2 15.1 %copy-start = (bf16[1,128,1024]{2,1,0:T(8,128)(2,1)S(1)}, bf16[1,128,1024]{2,1,0:T(8,128)(2,1)}, u32[]{:S(2)}) copy-start(bf16[1,128,1024]{2,1,0:T(8,128)(2,1)} %param.11) | copy-start | bytes 786436
  7.2 83.5 %all-gather.3.cloned.1.call-start = ((), (), s32[]{:S(2)}) async-start(), calls=%async_computation.4 | async-start | bytes 3342336 | tf_op jit(solution)/shard_map/all_gather | solution.py:192
  9.6 160.9 %reduce-scatter.2.cloned.1.call-start = ((), (), s32[]{:S(2)}) async-start(), calls=%async_computation.3 | async-start | bytes 3342336 | tf_op jit(solution)/shard_map/reduce_scatter | solution.py:211
  27.9 8.7 %copy-start.1 = (bf16[1,128,1024]{2,1,0:T(8,128)(2,1)S(1)}, bf16[1,128,1024]{2,1,0:T(8,128)(2,1)}, u32[]{:S(2)}) copy-start(bf16[1,128,1024]{2,1,0:T(8,128)(2,1)} %param.10) | copy-start | bytes 786436
  97.4 9.7 %copy-start.3 = (f32[1,128,8]{1,2,0:T(8,128)S(1)}, f32[1,128,8]{1,2,0:T(8,128)}, u32[]{:S(2)}) copy-start(f32[1,128,8]{1,2,0:T(8,128)} %param.14) | copy-start | bytes 12292
  102.5 20.0 %all-to-all-start.1 = ((bf16[8,64,1024]{2,1,0:T(8,128)(2,1)}), bf16[8,64,1024]{2,1,0:T(8,128)(2,1)S(1)}, u32[]{:S(2)}, u32[]{:S(2)}) async-start(bf16[8,64,1024]{2,1,0:T(8,128)(2,1)} %expert_forward.1), calls=%async_computation.1 | async-start | bytes 2097152 | tf_op jit(solution)/shard_map/all_to_all | solution.py:216
  129.4 3.0 %copy-start.2 = (bf16[1,128,1024]{2,1,0:T(8,128)(2,1)S(1)}, bf16[1,128,1024]{2,1,0:T(8,128)(2,1)}, u32[]{:S(2)}) copy-start(bf16[1,128,1024]{2,1,0:T(8,128)(2,1)} %param.12) | copy-start | bytes 786436
  132.7 14.5 %collective-permute-start.1 = (bf16[1,128,1024]{2,1,0:T(8,128)(2,1)S(1)}, bf16[1,128,1024]{2,1,0:T(8,128)(2,1)S(1)}, u32[]{:S(2)}, u32[]{:S(2)}) collective-permute-start(bf16[1,128,1024]{2,1,0:T(8,128)(2,1)S(1)} %fusion.23), channel_id=1, source_target_pairs={{0,384},{128,0},{256,128},{384,256},{1,385},{129,1},{257,129},{385... | collective-permute-start | bytes 786440 | tf_op jit(solution)/shard_map/ppermute | solution.py:22
  142.9 9.4 %collective-permute-start = (bf16[1,128,1024]{2,1,0:T(8,128)(2,1)S(1)}, bf16[1,128,1024]{2,1,0:T(8,128)(2,1)S(1)}, u32[]{:S(2)}, u32[]{:S(2)}) collective-permute-start(bf16[1,128,1024]{2,1,0:T(8,128)(2,1)S(1)} %fusion.17), channel_id=1, source_target_pairs={{0,128},{128,256},{256,384},{384,0},{1,129},{129,257},{257,385},{3... | collective-permute-start | bytes 786440 | tf_op jit(solution)/shard_map/ppermute | solution.py:22
Sparse Core Ops, SparseCore 0:
  10.6 79.9 all-gather.2
  97.1 73.4 reduce-scatter.1

commit v2 on v1

v2 whole, which is shorter than its diff:
```python
import functools
import math

import jax
import jax.numpy as jnp
from jax import lax
from jax.experimental import pallas as pl
from jax.experimental.pallas import tpu as pltpu
from jax.sharding import PartitionSpec as P

TOPK = 8
CAP = 32
EPSILON = 1e-06
F32 = jnp.float32
BF16 = jnp.bfloat16
CONTRACT_LAST = (((1,), (1,)), ((), ()))
CONTRACT_FIRST = (((0,), (0,)), ((), ()))
VMEM_LIMIT = 56 * 1024 * 1024


def from_behind(array, axis, by):
    size = lax.axis_size(axis)
    return lax.ppermute(array, axis, [(i, (i + by) % size) for i in range(size)])


def normalize(values):
    widened = values.astype(F32)
    factor = lax.rsqrt(jnp.mean(widened * widened, axis=-1, keepdims=True) + EPSILON)
    return (widened * factor, factor)


def slot_table(listed, window):
    hit_table = (listed[:, :, None] == jnp.arange(window, dtype=jnp.int32)[None, None, :]).astype(
        jnp.int32
    )
    flat_hits = hit_table.reshape(-1, window)
    before = jnp.cumsum(flat_hits, axis=0) - flat_hits
    ranked = jnp.sum(before * flat_hits, axis=1).reshape(listed.shape)
    return jnp.where(listed < window, listed * CAP + ranked, window * CAP)


def slot_owner(slot_ids, window):
    token_total = slot_ids.shape[0]
    token_index = jnp.repeat(jnp.arange(token_total, dtype=jnp.int32), slot_ids.shape[1])
    owners = (
        jnp.full((window * CAP + 1,), token_total, jnp.int32)
        .at[slot_ids.reshape(-1)]
        .set(token_index)
    )
    return owners[: window * CAP]


def slot_gates(slot_ids, gate_vals, window):
    filled = (
        jnp.zeros((window * CAP + 1,), F32).at[slot_ids.reshape(-1)].set(gate_vals.reshape(-1))
    )
    return filled[: window * CAP]


def pad_rows(row_table):
    extra = jnp.zeros((1, row_table.shape[-1]), row_table.dtype)
    return jnp.concatenate([row_table, extra], axis=0)


def dot(a, b):
    return jnp.dot(a, b, preferred_element_type=F32)


CHUNK = 4


def pack_body(gate_ref, up_ref, down_ref, own_ref):
    rows, half = gate_ref.shape
    own_ref[0:rows, 0:half] = gate_ref[...]
    own_ref[0:rows, half:] = up_ref[...]
    own_ref[rows:, :] = down_ref[...]


def unpack_body(scale, summed_ref, gate_ref, up_ref, down_ref):
    rows, half = gate_ref.shape
    gate_ref[...] = summed_ref[0:rows, 0:half].astype(F32) * scale
    up_ref[...] = summed_ref[0:rows, half:].astype(F32) * scale
    down_ref[...] = summed_ref[rows:, :].astype(F32) * scale


def land_body(a_ref, b_ref, x_ref, y_ref):
    x_ref[...] = a_ref[...]
    y_ref[...] = b_ref[...]


def backward_body(
    w_hbm, r_hbm, p_hbm, g_hbm, first_v, down_v, saved_v, grads_v, act_v, pd_v, pg_v, g_v, sem
):
    parts, block, width = w_hbm.shape
    half = width // 2
    rows = width // parts
    chunks = parts // CHUNK
    span = CHUNK * rows
    window = r_hbm.shape[0]
    slots = window * CAP
    load_saved = pltpu.make_async_copy(r_hbm.at[:, CAP : 2 * CAP, :], saved_v, sem.at[0])
    load_saved.start()
    loads = []
    for c in range(chunks):
        copy = pltpu.make_async_copy(
            w_hbm.at[c * CHUNK : (c + 1) * CHUNK, 0:rows, :], first_v.at[c], sem.at[3 + c]
        )
        copy.start()
        loads.append(copy)
    load_grads = pltpu.make_async_copy(r_hbm.at[:, 2 * CAP : 3 * CAP, :], grads_v, sem.at[1])
    load_grads.start()
    load_down = pltpu.make_async_copy(w_hbm.at[:, rows:block, :], down_v, sem.at[2])
    load_down.start()
    load_saved.wait()
    saved = saved_v[...].reshape(slots, width)
    for c in range(chunks):
        loads[c].wait()
        part = dot(saved[:, c * span : (c + 1) * span], first_v[c].reshape(span, width))
        act_v[...] = part if c == 0 else act_v[...] + part
    gate_act = act_v[:, :half]
    up_act = act_v[:, half:]
    sigma = jax.nn.sigmoid(gate_act)
    activated = gate_act * sigma
    hidden = (activated * up_act).astype(BF16)
    load_grads.wait()
    grads = grads_v[...].reshape(slots, width)
    p_down = lax.dot_general(hidden, grads, CONTRACT_FIRST, preferred_element_type=F32)
    pd_v[...] = p_down.astype(BF16).reshape(pd_v.shape)
    stores = [pltpu.make_async_copy(pd_v, p_hbm.at[:, rows:block, :], sem.at[3 + chunks])]
    stores[0].start()
    load_down.wait()
    down = down_v[...].reshape(half, width)
    grad_hidden = lax.dot_general(grads, down, CONTRACT_LAST, preferred_element_type=F32)
    grad_gate = (grad_hidden * up_act * sigma * (1.0 + gate_act * (1.0 - sigma))).astype(BF16)
    grad_up = (grad_hidden * activated).astype(BF16)
    g_v[:, :half] = grad_gate
    g_v[:, half:] = grad_up
    store_g = pltpu.make_async_copy(g_v, g_hbm, sem.at[4 + chunks])
    store_g.start()
    both = g_v[...]
    for c in range(chunks):
        part = lax.dot_general(
            saved[:, c * span : (c + 1) * span], both, CONTRACT_FIRST, preferred_element_type=F32
        )
        pg_v[c] = part.astype(BF16).reshape(CHUNK, rows, width)
        copy = pltpu.make_async_copy(
            pg_v.at[c], p_hbm.at[c * CHUNK : (c + 1) * CHUNK, 0:rows, :], sem.at[5 + chunks + c]
        )
        copy.start()
        stores.append(copy)
    store_g.wait()
    for copy in stores:
        copy.wait()


def forward_body(w_ref, r_ref, g_ref, o_ref):
    parts, block, width = w_ref.shape
    half = width // 2
    rows = width // parts
    window = r_ref.shape[0]
    first = w_ref[:, 0:rows, :].reshape(width, width)
    down = w_ref[:, rows:block, :].reshape(half, width)
    fresh = r_ref[:, 0:CAP, :].reshape(-1, width)
    act = dot(fresh, first)
    gate_act = act[:, :half]
    hidden = (gate_act * jax.nn.sigmoid(gate_act) * act[:, half:]).astype(BF16)
    o_ref[:, 0:CAP, :] = dot(hidden, down).astype(BF16).reshape(window, CAP, width)
    grad_input = lax.dot_general(g_ref[...], first, CONTRACT_LAST, preferred_element_type=F32)
    o_ref[:, CAP : 2 * CAP, :] = grad_input.astype(BF16).reshape(window, CAP, width)


def pack(gate, up, down):
    rows, half = gate.shape
    return pl.pallas_call(
        pack_body,
        out_shape=jax.ShapeDtypeStruct((rows + down.shape[0], 2 * half), BF16),
        name="pack_weights",
    )(gate, up, down)


def unpack(summed, rows, low, half, scale):
    return pl.pallas_call(
        functools.partial(unpack_body, scale),
        out_shape=(
            jax.ShapeDtypeStruct((rows, half), F32),
            jax.ShapeDtypeStruct((rows, half), F32),
            jax.ShapeDtypeStruct((low, 2 * half), F32),
        ),
        name="unpack_grads",
    )(summed)


def land(a, b):
    return pl.pallas_call(
        land_body,
        out_shape=(jax.ShapeDtypeStruct(a.shape, BF16), jax.ShapeDtypeStruct(b.shape, BF16)),
        cost_estimate=pl.CostEstimate(flops=0, bytes_accessed=1 << 20, transcendentals=0),
        name="land",
    )(a, b)


def expert_backward(gathered, received):
    parts, block, width = gathered.shape
    half = width // 2
    rows = width // parts
    chunks = parts // CHUNK
    window = received.shape[0]
    slots = window * CAP
    anywhere = pl.BlockSpec(memory_space=pl.ANY)
    return pl.pallas_call(
        backward_body,
        in_specs=[anywhere, anywhere],
        out_specs=(anywhere, anywhere),
        out_shape=(
            jax.ShapeDtypeStruct(gathered.shape, BF16),
            jax.ShapeDtypeStruct((slots, width), BF16),
        ),
        scratch_shapes=[
            pltpu.VMEM((chunks, CHUNK, rows, width), BF16),
            pltpu.VMEM((parts, block - rows, width), BF16),
            pltpu.VMEM((window, CAP, width), BF16),
            pltpu.VMEM((window, CAP, width), BF16),
            pltpu.VMEM((slots, width), F32),
            pltpu.VMEM((parts, block - rows, width), BF16),
            pltpu.VMEM((chunks, CHUNK, rows, width), BF16),
            pltpu.VMEM((slots, width), BF16),
            pltpu.SemaphoreType.DMA((5 + 2 * chunks,)),
        ],
        compiler_params=pltpu.CompilerParams(vmem_limit_bytes=VMEM_LIMIT),
        cost_estimate=pl.CostEstimate(
            flops=2 * slots * half * width * 6,
            bytes_accessed=8 * 1024 * 1024,
            transcendentals=slots * half,
        ),
        name="expert_backward",
    )(gathered, received)


def expert_forward(gathered, received, grads):
    width = gathered.shape[2]
    window = received.shape[0]
    slots = window * CAP
    return pl.pallas_call(
        forward_body,
        out_shape=jax.ShapeDtypeStruct((window, 2 * CAP, width), BF16),
        compiler_params=pltpu.CompilerParams(vmem_limit_bytes=VMEM_LIMIT),
        cost_estimate=pl.CostEstimate(
            flops=slots * width * width * 5,
            bytes_accessed=6 * 1024 * 1024,
            transcendentals=slots * width // 2,
        ),
        name="expert_forward",
    )(gathered, received, grads)


def local(
    section_input,
    saved_input,
    cotangent,
    routes_forward,
    gates_forward,
    routes_backward,
    gates_backward,
    gate_weight,
    up_weight,
    down_weight,
):
    window = lax.axis_size("expert")
    parts = lax.axis_size("dp")
    token_count = section_input.shape[1]
    model_width = section_input.shape[2]
    half = gate_weight.shape[3]
    rows = gate_weight.shape[2]
    low = down_weight.shape[2]

    own = pack(gate_weight[0, 0], up_weight[0, 0], down_weight[0, 0])
    gathered = lax.all_gather(own, "dp", axis=0, tiled=False)

    normed, _ = normalize(section_input[0])
    slot_ids = slot_table(routes_forward[0], window)
    owners = slot_owner(slot_ids, window)
    sent_forward = pad_rows(normed.astype(BF16))[owners].reshape(window, CAP, model_width)
    saved_float, saved_scale = normalize(saved_input[0])
    back_slots = slot_table(routes_backward[0], window)
    back_owners = slot_owner(back_slots, window)
    back_gates = slot_gates(back_slots, gates_backward[0], window)
    sent_backward = pad_rows(saved_float.astype(BF16))[back_owners].reshape(
        window, CAP, model_width
    )
    grad_sent = (back_gates[:, None] * pad_rows(cotangent[0])[back_owners].astype(F32)).astype(BF16)
    grad_sent = grad_sent.reshape(window, CAP, model_width)
    sent = jnp.concatenate([sent_forward, sent_backward, grad_sent], axis=1)
    received = lax.all_to_all(sent, "expert", split_axis=0, concat_axis=0, tiled=True)

    partial, act_grads = expert_backward(gathered, received)
    summed = lax.psum_scatter(
        partial.reshape(parts * (rows + low), model_width), "dp", scatter_dimension=0, tiled=True
    )

    produced = expert_forward(gathered, received, act_grads)
    home = lax.all_to_all(produced, "expert", split_axis=0, concat_axis=0, tiled=True)

    returned_pad = pad_rows(home[:, :CAP].reshape(window * CAP, model_width))
    mixed_sum = section_input[0].astype(F32)
    for slot_pos in range(TOPK):
        mixed_sum = mixed_sum + gates_forward[0][:, slot_pos, None] * returned_pad[
            slot_ids[:, slot_pos]
        ].astype(F32)
    handed = from_behind(mixed_sum.astype(BF16)[None], "section", 1)
    grad_pad = pad_rows(home[:, CAP:].reshape(window * CAP, model_width))
    token_grad = jnp.zeros((token_count, model_width), F32)
    for slot_pos in range(TOPK):
        token_grad = token_grad + grad_pad[back_slots[:, slot_pos]].astype(F32)
    mean_term = jnp.mean(saved_float * token_grad, axis=-1, keepdims=True)
    input_grad = cotangent[0].astype(F32) + saved_scale * (token_grad - saved_float * mean_term)
    grad_back = from_behind(input_grad.astype(BF16)[None], "section", -1)

    handed, grad_back = land(handed, grad_back)
    grad_scale = 1.0 / math.sqrt(parts * token_count)
    grad_gate, grad_up, grad_down = unpack(summed, rows, low, half, grad_scale)
    return (
        handed,
        grad_back,
        grad_gate[None, None],
        grad_up[None, None],
        grad_down[None, None],
    )


def solution(mesh):
    tokens = P("section", ("dp", "expert"), None)
    weights = P("section", "expert", "dp", None)
    return jax.shard_map(
        local,
        mesh=mesh,
        in_specs=(tokens,) * 7 + (weights,) * 3,
        out_specs=(tokens,) * 2 + (weights,) * 3,
        check_vma=False,
    )
```

time: 182 us -> 179 us (0.984)
  waiting for transfers between devices: 65.1 us -> 60.8 us
  Pallas kernels: 11.4 us -> 15.2 us
  other arithmetic: 13.1 us -> 10.4 us
    reduce_scatter x1, waiting for transfers between devices: 18.3 us -> 10.5 us  [local(): lax.psum_scatter(partial.reshape(parts * (rows + low), model_width), 'dp'...]
    gather x8, local copies, waits for them, and re-layouts: 8.29 us -> 12.5 us  [local(): token_grad = token_grad + grad_pad[back_slots[:, slot_pos]].astype(F32)]
    pallas_call x1 -> x4, Pallas kernels: 6.27 us -> 10.1 us  [the longest x1 4.91 us: expert_backward(): pl.pallas_call(backward_body, in_specs=[anywhere, anywhere], out_specs=(a...]
    ppermute x2, waiting for transfers between devices: 5.04 us -> 7.09 us  [from_behind(): lax.ppermute(array, axis, [(i, (i + by) % size) for i in range(size)])]
    unnamed x13 -> x15, local copies, waits for them, and re-layouts: 3.8 us -> 3.1 us
  transfers between devices with their start and end apart: 5 -> 5, of which waited for: 4 -> 5; matrix products, arithmetic and copies ran while one was open for 26% -> 28% of each run, Pallas kernels for 3% -> 4%
where the time goes in v2:
time: 179 us; the launch traced here: 178 us
  waiting for transfers between devices  60.8 us (34%)
  local copies, waits for them, and re-layouts  40.9 us (23%)
  blocking collectives  26 us (15%)
  Pallas kernels  15.2 us (8%)
  between operations  14.5 us (8%)
  starting transfers between devices  10.4 us (6%)
  other arithmetic  10.4 us (6%)
    all_gather x1, waiting for transfers between devices, local(): gathered = lax.all_gather(own, 'dp', axis=0, tiled=False)  27.7 us
    all_to_all x1, blocking collectives, local(): lax.all_to_all(sent, 'expert', split_axis=0, concat_axis=0, tiled=True)  26 us
    all_to_all x1, waiting for transfers between devices, local(): lax.all_to_all(produced, 'expert', split_axis=0, concat_axis=0, tiled=True)  15.5 us
    gather x8, local copies, waits for them, and re-layouts, local(): token_grad = token_grad + grad_pad[back_slots[:, slot_pos]].astype(F32)  12.5 us
    reduce_scatter x1, waiting for transfers between devices, local(): lax.psum_scatter(partial.reshape(parts * (rows + low), model_width), 'dp'...  10.5 us
    scatter x2, local copies, waits for them, and re-layouts, slot_owner(): owners = jnp.full((window * CAP + 1,), token_total, jnp.int32).at[slot_id...  8.61 us
    ppermute x2, waiting for transfers between devices, from_behind(): lax.ppermute(array, axis, [(i, (i + by) % size) for i in range(size)])  7.09 us
    gather x8, local copies, waits for them, and re-layouts, local(): returned_pad[slot_ids[:, slot_pos]].astype(F32)  6.88 us
  transfers between devices with their start and end apart: 5, of which 5 were waited for; matrix products, arithmetic and copies ran while one was open for 28% of the time, Pallas kernels for 4%

profile of v2, /device:TPU:6, one launch (start us, length us, event | category | flops | bytes accessed | tf_op | source)
XLA Modules:
  0.0 178.1 jit_solution(4494919344866594486)
XLA Ops:
  7.2 1.7 pack_weights.1
  9.0 0.8 copy.24
  9.8 0.1 eq.56
  9.9 0.8 copy.28
  10.7 0.1 eq.64
  10.9 2.3 %reduce-window.14 = s32[8,8,128]{2,1,0:T(8,128)S(1)} reduce-window(s32[8,8,128]{2,1,0:T(8,128)S(1)} %fusion.48, s32[]{:T(128)} %constant.9.clone.1), window={size=1x1x128 pad=0_0x0_0x127_0}, to_apply=%region_1.0 | reduce-window | flops 1040384 | bytes 65540 | tf_op jit(solution)/shard_map/reduce-window
  13.2 0.3 slice_reduce_fusion.1
  13.5 0.2 reduce-window.15
  13.7 2.3 %reduce-window.16 = s32[8,8,128]{2,1,0:T(8,128)S(1)} reduce-window(s32[8,8,128]{2,1,0:T(8,128)S(1)} %fusion.49, s32[]{:T(128)} %constant.9.clone.1), window={size=1x1x128 pad=0_0x0_0x127_0}, to_apply=%region_6.7 | reduce-window | flops 1040384 | bytes 65540 | tf_op jit(solution)/shard_map/reduce-window.2
  15.9 0.3 slice_reduce_fusion
  16.2 0.2 reduce-window.19
  16.6 0.1 mul.245
  16.7 0.1 lt.131
  17.0 0.1 mul.239
  17.1 0.1 lt.127
  17.2 0.8 copy.32
  18.1 4.3 %scatter_custom_fusion.2 = f32[257]{0:T(512)S(1)} fusion(s32[1024]{0:T(1024)S(1)} %bitcast.156, f32[1024]{0:T(1024)S(1)} %reshape.837, f32[]{:T(128)} %constant.11.clone.1), kind=kCustom, calls=%fused_computation.141 | custom fusion | bytes 1032 | tf_op jit(solution)/shard_map/scatter | solution.py:55
  22.5 0.1 reshape.829
  22.6 4.3 %scatter_custom_fusion.1 = s32[257]{0:T(512)S(1)} fusion(s32[1024]{0:T(1024)S(1)} %bitcast.157, s32[1024]{0:T(1024)S(1)} %reshape.829, s32[]{:T(128)} %constant.15.clone.1), kind=kCustom, calls=%fused_computation.143 | custom fusion | bytes 1032 | tf_op jit(solution)/shard_map/scatter | solution.py:48
  27.0 4.3 %scatter_custom_fusion = s32[257]{0:T(512)S(1)} fusion(s32[1024]{0:T(1024)S(1)} %bitcast.158, s32[1024]{0:T(1024)S(1)} %reshape.829, s32[]{:T(128)} %constant.15.clone.1), kind=kCustom, calls=%fused_computation.145 | custom fusion | bytes 1032 | tf_op jit(solution)/shard_map/scatter | solution.py:48
  31.3 1.1 fusion.8
  32.4 0.1 fusion.9
  32.5 0.1 fusion.18
  32.7 0.1 fusion.6
  32.9 1.2 gather_fusion.1
  34.1 1.2 gather_fusion.2
  35.3 1.2 gather_fusion
  36.4 0.2 fusion
  36.6 0.1 pad_maximum_fusion
  36.7 26.0 %all_to_all.10.r_hbm.r_ref = bf16[8,96,1024]{2,1,0:T(8,128)(2,1)} all-to-all(bf16[8,96,1024]{2,1,0:T(8,128)(2,1)S(1)} %pad_maximum_fusion), channel_id=1, replica_groups=mesh['section'=4,'dp'=16,'expert'=8] {'expert'}, dimensions={0} | all-to-all | bytes 3145728 | tf_op jit(solution)/shard_map/all_to_all | solution.py:293
  62.7 27.7 %all-gather.3.cloned.1.call-done = bf16[1536,1024]{1,0:T(8,128)(2,1)} async-done(((bf16[96,1024]{1,0:T(8,128)(2,1)}), bf16[1536,1024]{1,0:T(8,128)(2,1)}) %all-gather.3.cloned.1.call-update) | async-done | bytes 3145744 | tf_op jit(solution)/shard_map/all_gather | solution.py:277
  90.4 4.9 %expert_backward.1 = (bf16[16,96,1024]{2,1,0:T(8,128)(2,1)}, bf16[256,1024]{1,0:T(8,128)(2,1)}) custom-call(bf16[16,96,1024]{2,1,0:T(8,128)(2,1)} %bitcast.140, bf16[8,96,1024]{2,1,0:T(8,128)(2,1)} %all_to_all.10.r_hbm.r_ref), custom_call_target="tpu_custom_call" | custom-call | flops 1610612736 | bytes 8388608 | tf_op jit(solution)/shard_map/expert_backward/pallas_call | solution.py:210
  95.3 0.4 fusion.32
  95.7 5.1 %expert_forward.1 = bf16[8,64,1024]{2,1,0:T(8,128)(2,1)} custom-call(bf16[16,96,1024]{2,1,0:T(8,128)(2,1)} %bitcast.141, bf16[8,96,1024]{2,1,0:T(8,128)(2,1)} %all_to_all.10.r_hbm.r_ref, bf16[256,1024]{1,0:T(8,128)(2,1)} %get-tuple-element.12.g_ref), custom_call_target="tpu_custom_call" | custom-call | flops 1342177280 | bytes 6291456 | tf_op jit(solution)/shard_map/expert_forward/pallas_call | solution.py:243
  100.9 4.4 %all-to-all-start.1 = ((bf16[8,64,1024]{2,1,0:T(8,128)(2,1)}), bf16[8,64,1024]{2,1,0:T(8,128)(2,1)S(1)}, u32[]{:S(2)}, u32[]{:S(2)}) async-start(bf16[8,64,1024]{2,1,0:T(8,128)(2,1)} %expert_forward.1), calls=%async_computation.1 | async-start | bytes 2097152 | tf_op jit(solution)/shard_map/all_to_all | solution.py:301
  105.3 0.4 fusion.24
  105.8 15.5 %all-to-all-done.1 = bf16[8,64,1024]{2,1,0:T(8,128)(2,1)S(1)} async-done(((bf16[8,64,1024]{2,1,0:T(8,128)(2,1)}), bf16[8,64,1024]{2,1,0:T(8,128)(2,1)S(1)}, u32[]{:S(2)}, u32[]{:S(2)}) %all-to-all-start.1) | async-done | bytes 1048608 | tf_op jit(solution)/shard_map/all_to_all | solution.py:301
  121.4 1.6 gather_fusion.18
  123.0 1.6 gather_fusion.17
  124.5 1.6 gather_fusion.16
  126.1 1.6 gather_fusion.15
  127.7 1.6 gather_fusion.14
  129.3 1.6 gather_fusion.13
  130.8 1.5 gather_fusion.12
  132.4 1.6 gather_fusion.11
  133.9 0.9 gather_fusion.10
  134.8 0.9 gather_fusion.9
  135.7 0.9 gather_fusion.8
  136.5 0.9 gather_fusion.7
  137.4 0.9 gather_fusion.6
  138.2 0.9 gather_fusion.5
  139.1 0.9 gather_fusion.4
  140.0 0.9 gather_fusion.3
  140.8 0.5 fusion.17
  141.3 2.3 %collective-permute-start = (bf16[1,128,1024]{2,1,0:T(8,128)(2,1)S(1)}, bf16[1,128,1024]{2,1,0:T(8,128)(2,1)S(1)}, u32[]{:S(2)}, u32[]{:S(2)}) collective-permute-start(bf16[1,128,1024]{2,1,0:T(8,128)(2,1)S(1)} %fusion.17), channel_id=1, source_target_pairs={{0,128},{128,256},{256,384},{384,0},{1,129},{129,257},{257,385},{3... | collective-permute-start | bytes 786440 | tf_op jit(solution)/shard_map/ppermute | solution.py:23
  143.7 1.9 %fusion.7 = (f32[128]{0:T(128)S(1)}, f32[128,1024]{1,0:T(8,128)S(1)}) fusion(bf16[1,128,1024]{2,1,0:T(8,128)(2,1)S(1)} %copy-done, f32[128]{0:T(128)S(1)} %add_rsqrt_fusion, bf16[128,1024]{1,0:T(8,128)(2,1)} %gather_fusion.18, bf16[128,1024]{1,0:T(8,128)(2,1)} %gather_fusion.17, bf16[128,1024]{1,0:T(8,128)(2,1)} %gather_fusion.16, ...), kind=kLoop, calls=%fused_computation.35 | loop fusion | flops 2490240 | bytes 2884608 | tf_op jit(solution)/shard_map/reduce_sum | solution.py:314
  145.6 0.2 fusion.23
  145.9 3.5 %collective-permute-start.1 = (bf16[1,128,1024]{2,1,0:T(8,128)(2,1)S(1)}, bf16[1,128,1024]{2,1,0:T(8,128)(2,1)S(1)}, u32[]{:S(2)}, u32[]{:S(2)}) collective-permute-start(bf16[1,128,1024]{2,1,0:T(8,128)(2,1)S(1)} %fusion.23), channel_id=1, source_target_pairs={{0,384},{128,0},{256,128},{384,256},{1,385},{129,1},{257,129},{385... | collective-permute-start | bytes 786440 | tf_op jit(solution)/shard_map/ppermute | solution.py:23
  149.4 1.6 collective-permute-done.a_ref
  151.0 5.5 %collective-permute-done.1.b_ref = bf16[1,128,1024]{2,1,0:T(8,128)(2,1)S(1)} collective-permute-done((bf16[1,128,1024]{2,1,0:T(8,128)(2,1)S(1)}, bf16[1,128,1024]{2,1,0:T(8,128)(2,1)S(1)}, u32[]{:S(2)}, u32[]{:S(2)}) %collective-permute-start.1) | collective-permute-done | bytes 262176 | tf_op jit(solution)/shard_map/ppermute | solution.py:23
  156.5 0.7 copy-done.4
  157.2 1.8 %land.1 = (bf16[1,128,1024]{2,1,0:T(8,128)(2,1)}, bf16[1,128,1024]{2,1,0:T(8,128)(2,1)}) custom-call(bf16[1,128,1024]{2,1,0:T(8,128)(2,1)} %copy-done.3, bf16[1,128,1024]{2,1,0:T(8,128)(2,1)} %copy-done.4), custom_call_target="tpu_custom_call" | custom-call | bytes 1048576 | tf_op jit(solution)/shard_map/land/pallas_call | solution.py:194
  159.0 10.5 %reduce-scatter.2.cloned.1.call-done.summed_ref = bf16[96,1024]{1,0:T(8,128)(2,1)} async-done(((bf16[1536,1024]{1,0:T(8,128)(2,1)}), bf16[96,1024]{1,0:T(8,128)(2,1)}) %reduce-scatter.2.cloned.1.call-update) | async-done | bytes 196624 | tf_op jit(solution)/shard_map/reduce_scatter | solution.py:296
  169.5 1.7 unpack_grads.1
  (57 shorter events, 1.3 us)
Async XLA Ops:
  7.2 25.2 %copy-start.1 = (bf16[1,128,1024]{2,1,0:T(8,128)(2,1)S(1)}, bf16[1,128,1024]{2,1,0:T(8,128)(2,1)}, u32[]{:S(2)}) copy-start(bf16[1,128,1024]{2,1,0:T(8,128)(2,1)} %param.10) | copy-start | bytes 786436
  7.2 25.4 %copy-start = (bf16[1,128,1024]{2,1,0:T(8,128)(2,1)S(1)}, bf16[1,128,1024]{2,1,0:T(8,128)(2,1)}, u32[]{:S(2)}) copy-start(bf16[1,128,1024]{2,1,0:T(8,128)(2,1)} %param.11) | copy-start | bytes 786436
  7.2 25.7 %copy-start.2 = (bf16[1,128,1024]{2,1,0:T(8,128)(2,1)S(1)}, bf16[1,128,1024]{2,1,0:T(8,128)(2,1)}, u32[]{:S(2)}) copy-start(bf16[1,128,1024]{2,1,0:T(8,128)(2,1)} %param.12) | copy-start | bytes 786436
  7.2 83.2 %all-gather.3.cloned.1.call-start = ((), (), s32[]{:S(2)}) async-start(), calls=%async_computation.4 | async-start | bytes 3342336 | tf_op jit(solution)/shard_map/all_gather | solution.py:277
  8.9 160.6 %reduce-scatter.2.cloned.1.call-start = ((), (), s32[]{:S(2)}) async-start(), calls=%async_computation.3 | async-start | bytes 3342336 | tf_op jit(solution)/shard_map/reduce_scatter | solution.py:296
  95.7 10.0 %copy-start.5 = (f32[1,128,8]{1,2,0:T(8,128)S(1)}, f32[1,128,8]{1,2,0:T(8,128)}, u32[]{:S(2)}) copy-start(f32[1,128,8]{1,2,0:T(8,128)} %param.14) | copy-start | bytes 12292
  100.9 20.4 %all-to-all-start.1 = ((bf16[8,64,1024]{2,1,0:T(8,128)(2,1)}), bf16[8,64,1024]{2,1,0:T(8,128)(2,1)S(1)}, u32[]{:S(2)}, u32[]{:S(2)}) async-start(bf16[8,64,1024]{2,1,0:T(8,128)(2,1)} %expert_forward.1), calls=%async_computation.1 | async-start | bytes 2097152 | tf_op jit(solution)/shard_map/all_to_all | solution.py:301
  141.3 9.6 %collective-permute-start = (bf16[1,128,1024]{2,1,0:T(8,128)(2,1)S(1)}, bf16[1,128,1024]{2,1,0:T(8,128)(2,1)S(1)}, u32[]{:S(2)}, u32[]{:S(2)}) collective-permute-start(bf16[1,128,1024]{2,1,0:T(8,128)(2,1)S(1)} %fusion.17), channel_id=1, source_target_pairs={{0,128},{128,256},{256,384},{384,0},{1,129},{129,257},{257,385},{3... | collective-permute-start | bytes 786440 | tf_op jit(solution)/shard_map/ppermute | solution.py:23
  145.9 10.6 %collective-permute-start.1 = (bf16[1,128,1024]{2,1,0:T(8,128)(2,1)S(1)}, bf16[1,128,1024]{2,1,0:T(8,128)(2,1)S(1)}, u32[]{:S(2)}, u32[]{:S(2)}) collective-permute-start(bf16[1,128,1024]{2,1,0:T(8,128)(2,1)S(1)} %fusion.23), channel_id=1, source_target_pairs={{0,384},{128,0},{256,128},{384,256},{1,385},{129,1},{257,129},{385... | collective-permute-start | bytes 786440 | tf_op jit(solution)/shard_map/ppermute | solution.py:23
  151.0 5.5 %copy-start.3 = (bf16[1,128,1024]{2,1,0:T(8,128)(2,1)}, bf16[1,128,1024]{2,1,0:T(8,128)(2,1)S(1)}, u32[]{:S(2)}) copy-start(bf16[1,128,1024]{2,1,0:T(8,128)(2,1)S(1)} %collective-permute-done.a_ref) | copy-start | bytes 786436
  156.5 0.7 copy-start.4
Sparse Core Ops, SparseCore 0:
  10.7 79.6 all-gather.2
  95.4 74.0 reduce-scatter.1

commit v3 on v2

--- a/solution.py
+++ b/solution.py
@@ -21,6 +21,23 @@
 def from_behind(array, axis, by):
     size = lax.axis_size(axis)
     return lax.ppermute(array, axis, [(i, (i + by) % size) for i in range(size)])
+
+
+def crossed(expert, index):
+    return expert ^ (index & 1)
+
+
+def cross_rings():
+    parts, window = lax.axis_size("dp"), lax.axis_size("expert")
+    return [[d * window + crossed(e, d) for d in range(parts)] for e in range(window)]
+
+
+def cross_swap(array):
+    parts, window = lax.axis_size("dp"), lax.axis_size("expert")
+    pairs = [
+        (d * window + e, d * window + crossed(e, d)) for d in range(parts) for e in range(window)
+    ]
+    return lax.ppermute(array, ("dp", "expert"), pairs)
 
 
 def normalize(values):
@@ -186,6 +203,7 @@
             jax.ShapeDtypeStruct((rows, half), F32),
             jax.ShapeDtypeStruct((low, 2 * half), F32),
         ),
+        compiler_params=pltpu.CompilerParams(vmem_limit_bytes=8 * 1024 * 1024),
         name="unpack_grads",
     )(summed)
 
@@ -274,14 +292,35 @@
     low = down_weight.shape[2]
 
     own = pack(gate_weight[0, 0], up_weight[0, 0], down_weight[0, 0])
-    gathered = lax.all_gather(own, "dp", axis=0, tiled=False)
+    index = lax.axis_index("dp")
+    own = cross_swap(own)
+    own, section_input, saved_input, cotangent, routes_forward, routes_backward, gates_backward = (
+        lax.optimization_barrier(
+            (
+                own,
+                section_input,
+                saved_input,
+                cotangent,
+                routes_forward,
+                routes_backward,
+                gates_backward,
+            )
+        )
+    )
+    gathered = lax.all_gather(
+        own,
+        ("dp", "expert"),
+        axis=0,
+        tiled=True,
+        axis_index_groups=cross_rings(),
+    ).reshape(parts, rows + low, model_width)
 
     normed, _ = normalize(section_input[0])
-    slot_ids = slot_table(routes_forward[0], window)
+    slot_ids = slot_table(crossed(routes_forward[0], index), window)
     owners = slot_owner(slot_ids, window)
     sent_forward = pad_rows(normed.astype(BF16))[owners].reshape(window, CAP, model_width)
     saved_float, saved_scale = normalize(saved_input[0])
-    back_slots = slot_table(routes_backward[0], window)
+    back_slots = slot_table(crossed(routes_backward[0], index), window)
     back_owners = slot_owner(back_slots, window)
     back_gates = slot_gates(back_slots, gates_backward[0], window)
     sent_backward = pad_rows(saved_float.astype(BF16))[back_owners].reshape(
@@ -294,7 +333,11 @@
 
     partial, act_grads = expert_backward(gathered, received)
     summed = lax.psum_scatter(
-        partial.reshape(parts * (rows + low), model_width), "dp", scatter_dimension=0, tiled=True
+        partial.reshape(parts * (rows + low), model_width),
+        ("dp", "expert"),
+        scatter_dimension=0,
+        axis_index_groups=cross_rings(),
+        tiled=True,
     )
 
     produced = expert_forward(gathered, received, act_grads)
@@ -316,6 +359,8 @@
     grad_back = from_behind(input_grad.astype(BF16)[None], "section", -1)
 
     handed, grad_back = land(handed, grad_back)
+    summed, handed, grad_back = lax.optimization_barrier((summed, handed, grad_back))
+    summed = cross_swap(summed)
     grad_scale = 1.0 / math.sqrt(parts * token_count)
     grad_gate, grad_up, grad_down = unpack(summed, rows, low, half, grad_scale)
     return (

time: 179 us -> 173 us (0.966)
  waiting for transfers between devices: 60.8 us -> 55.8 us
  local copies, waits for them, and re-layouts: 40.9 us -> 37.6 us
  starting transfers between devices: 10.4 us -> 13.6 us
    all_gather x1, waiting for transfers between devices: 27.7 us -> 21.6 us  [local(): lax.all_gather(own, ('dp', 'expert'), axis=0, tiled=True, axis_index_grou...]
    gather x8, local copies, waits for them, and re-layouts: 12.5 us -> 6.89 us  [local(): token_grad = token_grad + grad_pad[back_slots[:, slot_pos]].astype(F32)]
    ppermute x0 -> x2, starting transfers between devices: none -> 3.15 us  [cross_swap(): return lax.ppermute(array, ('dp', 'expert'), pairs)]
    optimization_barrier x0 -> x3, local copies, waits for them, and re-layouts: none -> 2.36 us  [local(): lax.optimization_barrier((own, section_input, saved_input, cotangent, rou...]
  transfers between devices with their start and end apart: 5 -> 7, of which waited for: 5 -> 4; matrix products, arithmetic and copies ran while one was open for 28% -> 27% of each run, Pallas kernels for 4% -> 4%
where the time goes in v3:
time: 173 us; the launch traced here: 172 us
  waiting for transfers between devices  55.8 us (32%)
  local copies, waits for them, and re-layouts  37.6 us (22%)
  blocking collectives  26 us (15%)
  between operations  14.5 us (8%)
  Pallas kernels  14.3 us (8%)
  starting transfers between devices  13.6 us (8%)
  other arithmetic  9.77 us (6%)
    all_to_all x1, blocking collectives, local(): lax.all_to_all(sent, 'expert', split_axis=0, concat_axis=0, tiled=True)  26 us
    all_gather x1, waiting for transfers between devices, local(): lax.all_gather(own, ('dp', 'expert'), axis=0, tiled=True, axis_index_grou...  21.6 us
    all_to_all x1, waiting for transfers between devices, local(): lax.all_to_all(produced, 'expert', split_axis=0, concat_axis=0, tiled=True)  15.8 us
    reduce_scatter x1, waiting for transfers between devices, local(): lax.psum_scatter(partial.reshape(parts * (rows + low), model_width), ('dp...  11.1 us
    scatter x2, local copies, waits for them, and re-layouts, slot_owner(): owners = jnp.full((window * CAP + 1,), token_total, jnp.int32).at[slot_id...  8.61 us
    gather x8, local copies, waits for them, and re-layouts, local(): returned_pad[slot_ids[:, slot_pos]].astype(F32)  7.59 us
    ppermute x2, waiting for transfers between devices, from_behind(): lax.ppermute(array, axis, [(i, (i + by) % size) for i in range(size)])  7.22 us
    gather x8, local copies, waits for them, and re-layouts, local(): token_grad = token_grad + grad_pad[back_slots[:, slot_pos]].astype(F32)  6.89 us
  transfers between devices with their start and end apart: 7, of which 4 were waited for; matrix products, arithmetic and copies ran while one was open for 27% of the time, Pallas kernels for 4%

profile of v3, /device:TPU:6, one launch (start us, length us, event | category | flops | bytes accessed | tf_op | source)
XLA Modules:
  0.0 171.5 jit_solution(7847533652048974261)
XLA Ops:
  7.2 1.6 pack_weights.1
  8.9 1.6 collective-permute-start
  10.5 0.1 reshape.851
  10.6 0.7 copy-done.4
  11.3 0.8 copy.19
  12.1 0.8 copy.18
  13.3 2.3 %reduce-window.16 = s32[8,8,128]{2,1,0:T(8,128)S(1)} reduce-window(s32[8,8,128]{2,1,0:T(8,128)S(1)} %fusion.49, s32[]{:T(128)} %constant.40.clone.1), window={size=1x1x128 pad=0_0x0_0x127_0}, to_apply=%region_6.7 | reduce-window | flops 1040384 | bytes 65540 | tf_op jit(solution)/shard_map/reduce-window.2
  15.6 0.3 slice_reduce_fusion
  15.9 0.2 reduce-window.19
  16.2 0.1 lt.131
  16.3 0.1 mul.243
  16.4 0.8 copy.20
  17.3 4.3 %scatter_custom_fusion.2 = f32[257]{0:T(512)S(1)} fusion(s32[1024]{0:T(1024)S(1)} %bitcast.153, f32[1024]{0:T(1024)S(1)} %reshape.859, f32[]{:T(128)} %constant.14.clone.1), kind=kCustom, calls=%fused_computation.143 | custom fusion | bytes 1032 | tf_op jit(solution)/shard_map/scatter | solution.py:72
  21.7 1.0 concatenate.20
  22.7 1.1 fusion.18
  23.8 0.1 fusion.6
  24.0 4.3 %scatter_custom_fusion.1 = s32[257]{0:T(512)S(1)} fusion(s32[1024]{0:T(1024)S(1)} %bitcast.154, s32[1024]{0:T(1024)S(1)} %reshape.851, s32[]{:T(128)} %constant.18.clone.1), kind=kCustom, calls=%fused_computation.145 | custom fusion | bytes 1032 | tf_op jit(solution)/shard_map/scatter | solution.py:65
  28.3 1.2 gather_fusion.2
  29.5 1.2 gather_fusion.1
  30.7 0.1 fusion.9
  30.8 2.3 %reduce-window.14 = s32[8,8,128]{2,1,0:T(8,128)S(1)} reduce-window(s32[8,8,128]{2,1,0:T(8,128)S(1)} %fusion.48, s32[]{:T(128)} %constant.40.clone.1), window={size=1x1x128 pad=0_0x0_0x127_0}, to_apply=%region_1.0 | reduce-window | flops 1040384 | bytes 65540 | tf_op jit(solution)/shard_map/reduce-window
  33.1 0.3 slice_reduce_fusion.1
  33.4 0.2 reduce-window.15
  33.8 0.1 lt.127
  33.9 0.1 mul.237
  34.0 4.3 %scatter_custom_fusion = s32[257]{0:T(512)S(1)} fusion(s32[1024]{0:T(1024)S(1)} %bitcast.155, s32[1024]{0:T(1024)S(1)} %reshape.851, s32[]{:T(128)} %constant.18.clone.1), kind=kCustom, calls=%fused_computation.147 | custom fusion | bytes 1032 | tf_op jit(solution)/shard_map/scatter | solution.py:65
  38.3 1.2 gather_fusion
  39.5 0.2 fusion
  39.7 0.1 pad_maximum_fusion
  39.8 26.0 %all_to_all.10.r_hbm.r_ref = bf16[8,96,1024]{2,1,0:T(8,128)(2,1)} all-to-all(bf16[8,96,1024]{2,1,0:T(8,128)(2,1)S(1)} %pad_maximum_fusion), channel_id=1, replica_groups=mesh['section'=4,'dp'=16,'expert'=8] {'expert'}, dimensions={0} | all-to-all | bytes 3145728 | tf_op jit(solution)/shard_map/all_to_all | solution.py:332
  65.8 21.6 %all-gather.2.cloned.1.call-done = bf16[1536,1024]{1,0:T(8,128)(2,1)} async-done(((bf16[96,1024]{1,0:T(8,128)(2,1)}), bf16[1536,1024]{1,0:T(8,128)(2,1)}) %all-gather.2.cloned.1.call-update) | async-done | bytes 3145744 | tf_op jit(solution)/shard_map/all_gather | solution.py:310
  87.4 4.9 %expert_backward.1 = (bf16[16,96,1024]{2,1,0:T(8,128)(2,1)}, bf16[256,1024]{1,0:T(8,128)(2,1)}) custom-call(bf16[16,96,1024]{2,1,0:T(8,128)(2,1)} %bitcast.136, bf16[8,96,1024]{2,1,0:T(8,128)(2,1)} %all_to_all.10.r_hbm.r_ref), custom_call_target="tpu_custom_call" | custom-call | flops 1610612736 | bytes 8388608 | tf_op jit(solution)/shard_map/expert_backward/pallas_call | solution.py:228
  92.3 0.4 fusion.24
  92.8 0.4 fusion.32
  93.2 5.1 %expert_forward.1 = bf16[8,64,1024]{2,1,0:T(8,128)(2,1)} custom-call(bf16[16,96,1024]{2,1,0:T(8,128)(2,1)} %bitcast.137, bf16[8,96,1024]{2,1,0:T(8,128)(2,1)} %all_to_all.10.r_hbm.r_ref, bf16[256,1024]{1,0:T(8,128)(2,1)} %get-tuple-element.30.g_ref), custom_call_target="tpu_custom_call" | custom-call | flops 1342177280 | bytes 6291456 | tf_op jit(solution)/shard_map/expert_forward/pallas_call | solution.py:261
  98.3 4.5 %all-to-all-start.1 = ((bf16[8,64,1024]{2,1,0:T(8,128)(2,1)}), bf16[8,64,1024]{2,1,0:T(8,128)(2,1)S(1)}, u32[]{:S(2)}, u32[]{:S(2)}) async-start(bf16[8,64,1024]{2,1,0:T(8,128)(2,1)} %expert_forward.1), calls=%async_computation.2 | async-start | bytes 2097152 | tf_op jit(solution)/shard_map/all_to_all | solution.py:344
  103.0 15.8 %all-to-all-done.1 = bf16[8,64,1024]{2,1,0:T(8,128)(2,1)S(1)} async-done(((bf16[8,64,1024]{2,1,0:T(8,128)(2,1)}), bf16[8,64,1024]{2,1,0:T(8,128)(2,1)S(1)}, u32[]{:S(2)}, u32[]{:S(2)}) %all-to-all-start.1) | async-done | bytes 1048608 | tf_op jit(solution)/shard_map/all_to_all | solution.py:344
  118.9 0.9 gather_fusion.10
  119.8 0.9 gather_fusion.9
  120.6 0.9 gather_fusion.8
  121.5 0.9 gather_fusion.7
  122.4 0.9 gather_fusion.6
  123.2 0.9 gather_fusion.5
  124.1 0.9 gather_fusion.4
  125.0 1.6 gather_fusion.3
  126.5 1.5 fusion.17
  128.0 2.5 %collective-permute-start.1 = (bf16[1,128,1024]{2,1,0:T(8,128)(2,1)S(1)}, bf16[1,128,1024]{2,1,0:T(8,128)(2,1)}, u32[]{:S(2)}, u32[]{:S(2)}) collective-permute-start(bf16[1,128,1024]{2,1,0:T(8,128)(2,1)S(1)} %fusion.17), channel_id=1, source_target_pairs={{0,128},{128,256},{256,384},{384,0},{1,129},{129,257},{257,385},{3... | collective-permute-start | bytes 786440 | tf_op jit(solution)/shard_map/ppermute | solution.py:23
  130.5 0.9 gather_fusion.18
  131.4 0.9 gather_fusion.17
  132.3 0.9 gather_fusion.16
  133.1 0.9 gather_fusion.15
  134.0 0.9 gather_fusion.14
  134.8 0.9 gather_fusion.13
  135.7 0.9 gather_fusion.12
  136.6 0.9 gather_fusion.11
  137.4 0.4 fusion.7
  137.9 0.2 fusion.23
  138.1 3.3 %collective-permute-start.2 = (bf16[1,128,1024]{2,1,0:T(8,128)(2,1)S(1)}, bf16[1,128,1024]{2,1,0:T(8,128)(2,1)S(1)}, u32[]{:S(2)}, u32[]{:S(2)}) collective-permute-start(bf16[1,128,1024]{2,1,0:T(8,128)(2,1)S(1)} %fusion.23), channel_id=1, source_target_pairs={{0,384},{128,0},{256,128},{384,256},{1,385},{129,1},{257,129},{385... | collective-permute-start | bytes 786440 | tf_op jit(solution)/shard_map/ppermute | solution.py:23
  141.5 7.2 %collective-permute-done.2.b_ref = bf16[1,128,1024]{2,1,0:T(8,128)(2,1)S(1)} collective-permute-done((bf16[1,128,1024]{2,1,0:T(8,128)(2,1)S(1)}, bf16[1,128,1024]{2,1,0:T(8,128)(2,1)S(1)}, u32[]{:S(2)}, u32[]{:S(2)}) %collective-permute-start.2) | collective-permute-done | bytes 262176 | tf_op jit(solution)/shard_map/ppermute | solution.py:23
  148.7 0.7 copy-done.3
  149.4 1.8 %land.1 = (bf16[1,128,1024]{2,1,0:T(8,128)(2,1)}, bf16[1,128,1024]{2,1,0:T(8,128)(2,1)}) custom-call(bf16[1,128,1024]{2,1,0:T(8,128)(2,1)} %collective-permute-done.1.a_ref, bf16[1,128,1024]{2,1,0:T(8,128)(2,1)} %copy-done.3), custom_call_target="tpu_custom_call" | custom-call | bytes 1048576 | tf_op jit(solution)/shard_map/land/pallas_call | solution.py:212
  151.2 11.1 %reduce-scatter.2.cloned.1.call-done = bf16[96,1024]{1,0:T(8,128)(2,1)} async-done(((bf16[1536,1024]{1,0:T(8,128)(2,1)}), bf16[96,1024]{1,0:T(8,128)(2,1)}) %reduce-scatter.2.cloned.1.call-update) | async-done | bytes 196624 | tf_op jit(solution)/shard_map/reduce_scatter | solution.py:335
  162.3 1.6 collective-permute-start.3
  163.9 0.8 unpack_grads.1
  (67 shorter events, 1.5 us)
Async XLA Ops:
  7.2 16.6 %copy-start.1 = (bf16[1,128,1024]{2,1,0:T(8,128)(2,1)S(1)}, bf16[1,128,1024]{2,1,0:T(8,128)(2,1)}, u32[]{:S(2)}) copy-start(bf16[1,128,1024]{2,1,0:T(8,128)(2,1)} %param.10) | copy-start | bytes 786436
  7.2 16.6 %copy-start = (bf16[1,128,1024]{2,1,0:T(8,128)(2,1)S(1)}, bf16[1,128,1024]{2,1,0:T(8,128)(2,1)}, u32[]{:S(2)}) copy-start(bf16[1,128,1024]{2,1,0:T(8,128)(2,1)} %param.11) | copy-start | bytes 786436
  7.2 80.2 %all-gather.2.cloned.1.call-start = ((), (), s32[]{:S(2)}) async-start(), calls=%async_computation.3 | async-start | bytes 3342336 | tf_op jit(solution)/shard_map/all_gather | solution.py:310
  8.9 1.7 collective-permute-start
  10.6 0.7 copy-start.4
  11.3 151.1 %reduce-scatter.2.cloned.1.call-start = ((), (), s32[]{:S(2)}) async-start(), calls=%async_computation.4 | async-start | bytes 3342336 | tf_op jit(solution)/shard_map/reduce_scatter | solution.py:335
  87.4 5.0 %copy-start.5 = (f32[1,128,8]{1,2,0:T(8,128)S(1)}, f32[1,128,8]{1,2,0:T(8,128)}, u32[]{:S(2)}) copy-start(f32[1,128,8]{1,2,0:T(8,128)} %param.14) | copy-start | bytes 12292
  98.3 20.4 %all-to-all-start.1 = ((bf16[8,64,1024]{2,1,0:T(8,128)(2,1)}), bf16[8,64,1024]{2,1,0:T(8,128)(2,1)S(1)}, u32[]{:S(2)}, u32[]{:S(2)}) async-start(bf16[8,64,1024]{2,1,0:T(8,128)(2,1)} %expert_forward.1), calls=%async_computation.2 | async-start | bytes 2097152 | tf_op jit(solution)/shard_map/all_to_all | solution.py:344
  128.0 13.5 %collective-permute-start.1 = (bf16[1,128,1024]{2,1,0:T(8,128)(2,1)S(1)}, bf16[1,128,1024]{2,1,0:T(8,128)(2,1)}, u32[]{:S(2)}, u32[]{:S(2)}) collective-permute-start(bf16[1,128,1024]{2,1,0:T(8,128)(2,1)S(1)} %fusion.17), channel_id=1, source_target_pairs={{0,128},{128,256},{256,384},{384,0},{1,129},{129,257},{257,385},{3... | collective-permute-start | bytes 786440 | tf_op jit(solution)/shard_map/ppermute | solution.py:23
  136.6 1.3 copy-start.2
  138.1 10.6 %collective-permute-start.2 = (bf16[1,128,1024]{2,1,0:T(8,128)(2,1)S(1)}, bf16[1,128,1024]{2,1,0:T(8,128)(2,1)S(1)}, u32[]{:S(2)}, u32[]{:S(2)}) collective-permute-start(bf16[1,128,1024]{2,1,0:T(8,128)(2,1)S(1)} %fusion.23), channel_id=1, source_target_pairs={{0,384},{128,0},{256,128},{384,256},{1,385},{129,1},{257,129},{385... | collective-permute-start | bytes 786440 | tf_op jit(solution)/shard_map/ppermute | solution.py:23
  148.7 0.7 copy-start.3
  162.3 1.6 collective-permute-start.3
Sparse Core Ops, SparseCore 0:
  11.4 75.9 all-gather.1
  92.4 69.8 reduce-scatter.1

commit v4 on v3

--- a/solution.py
+++ b/solution.py
@@ -24,7 +24,8 @@
 
 
 def crossed(expert, index):
-    return expert ^ (index & 1)
+    half = lax.axis_size("dp") // 2
+    return expert ^ (1 - index // half)
 
 
 def cross_rings():

time: 173 us -> 182 us (1.052)
  waiting for transfers between devices: 55.8 us -> 60.5 us
  starting transfers between devices: 13.6 us -> 17.4 us
    ppermute x2, starting transfers between devices: 3.15 us -> 6.41 us  [cross_swap(): return lax.ppermute(array, ('dp', 'expert'), pairs)]
    ppermute x2, waiting for transfers between devices: 0.01 us -> 2.75 us  [cross_swap(): return lax.ppermute(array, ('dp', 'expert'), pairs)]
  transfers between devices with their start and end apart: 7 -> 7, of which waited for: 4 -> 6; matrix products, arithmetic and copies ran while one was open for 27% -> 26% of each run, Pallas kernels for 4% -> 4%
where the time goes in v4:
time: 182 us; the launch traced here: 180 us
  waiting for transfers between devices  60.5 us (33%)
  local copies, waits for them, and re-layouts  37.6 us (21%)
  blocking collectives  26 us (14%)
  starting transfers between devices  17.4 us (10%)
  between operations  14.5 us (8%)
  Pallas kernels  14.3 us (8%)
  other arithmetic  9.77 us (5%)
    all_to_all x1, blocking collectives, local(): lax.all_to_all(sent, 'expert', split_axis=0, concat_axis=0, tiled=True)  26 us
    all_gather x1, waiting for transfers between devices, local(): lax.all_gather(own, ('dp', 'expert'), axis=0, tiled=True, axis_index_grou...  22.2 us
    all_to_all x1, waiting for transfers between devices, local(): lax.all_to_all(produced, 'expert', split_axis=0, concat_axis=0, tiled=True)  15.8 us
    reduce_scatter x1, waiting for transfers between devices, local(): lax.psum_scatter(partial.reshape(parts * (rows + low), model_width), ('dp...  12.6 us
    scatter x2, local copies, waits for them, and re-layouts, slot_owner(): owners = jnp.full((window * CAP + 1,), token_total, jnp.int32).at[slot_id...  8.61 us
    gather x8, local copies, waits for them, and re-layouts, local(): returned_pad[slot_ids[:, slot_pos]].astype(F32)  7.59 us
    ppermute x2, waiting for transfers between devices, from_behind(): lax.ppermute(array, axis, [(i, (i + by) % size) for i in range(size)])  7.05 us
    gather x8, local copies, waits for them, and re-layouts, local(): token_grad = token_grad + grad_pad[back_slots[:, slot_pos]].astype(F32)  6.89 us
  transfers between devices with their start and end apart: 7, of which 6 were waited for; matrix products, arithmetic and copies ran while one was open for 26% of the time, Pallas kernels for 4%

profile of v4, /device:TPU:6, one launch (start us, length us, event | category | flops | bytes accessed | tf_op | source)
XLA Modules:
  0.0 180.1 jit_solution(24670363140996617)
XLA Ops:
  7.2 1.6 pack_weights.1
  8.9 1.9 %collective-permute-start = (bf16[96,1024]{1,0:T(8,128)(2,1)}, bf16[96,1024]{1,0:T(8,128)(2,1)S(1)}, u32[]{:S(2)}, u32[]{:S(2)}) collective-permute-start(bf16[96,1024]{1,0:T(8,128)(2,1)} %pack_weights.1), channel_id=1, source_target_pairs={{0,1},{1,0},{2,3},{3,2},{4,5},{5,4},{6,7},{7,6},{8,9},{9,8},{10,11... | collective-permute-start | bytes 589832 | tf_op jit(solution)/shard_map/ppermute | solution.py:41
  10.9 1.5 collective-permute-done
  12.4 0.7 copy-done.4
  13.2 0.8 copy.19
  13.9 0.8 copy.18
  15.1 2.3 %reduce-window.16 = s32[8,8,128]{2,1,0:T(8,128)S(1)} reduce-window(s32[8,8,128]{2,1,0:T(8,128)S(1)} %fusion.49, s32[]{:T(128)} %constant.51.clone.1), window={size=1x1x128 pad=0_0x0_0x127_0}, to_apply=%region_6.7 | reduce-window | flops 1040384 | bytes 65540 | tf_op jit(solution)/shard_map/reduce-window.2
  17.4 0.3 slice_reduce_fusion
  17.7 0.2 reduce-window.19
  18.1 0.1 lt.131
  18.2 0.1 mul.243
  18.3 0.8 copy.20
  19.2 4.3 %scatter_custom_fusion.2 = f32[257]{0:T(512)S(1)} fusion(s32[1024]{0:T(1024)S(1)} %bitcast.153, f32[1024]{0:T(1024)S(1)} %reshape.859, f32[]{:T(128)} %constant.20.clone.1), kind=kCustom, calls=%fused_computation.143 | custom fusion | bytes 1032 | tf_op jit(solution)/shard_map/scatter | solution.py:73
  23.6 1.0 concatenate.20
  24.6 1.1 fusion.18
  25.7 0.1 fusion.6
  25.8 4.3 %scatter_custom_fusion.1 = s32[257]{0:T(512)S(1)} fusion(s32[1024]{0:T(1024)S(1)} %bitcast.154, s32[1024]{0:T(1024)S(1)} %reshape.851, s32[]{:T(128)} %constant.47.clone.1), kind=kCustom, calls=%fused_computation.145 | custom fusion | bytes 1032 | tf_op jit(solution)/shard_map/scatter | solution.py:66
  30.2 1.2 gather_fusion.2
  31.3 1.2 gather_fusion.1
  32.5 0.1 fusion.9
  32.7 2.3 %reduce-window.14 = s32[8,8,128]{2,1,0:T(8,128)S(1)} reduce-window(s32[8,8,128]{2,1,0:T(8,128)S(1)} %fusion.48, s32[]{:T(128)} %constant.51.clone.1), window={size=1x1x128 pad=0_0x0_0x127_0}, to_apply=%region_1.2 | reduce-window | flops 1040384 | bytes 65540 | tf_op jit(solution)/shard_map/reduce-window
  35.0 0.3 slice_reduce_fusion.1
  35.2 0.2 reduce-window.15
  35.6 0.1 lt.127
  35.9 4.3 %scatter_custom_fusion = s32[257]{0:T(512)S(1)} fusion(s32[1024]{0:T(1024)S(1)} %bitcast.155, s32[1024]{0:T(1024)S(1)} %reshape.851, s32[]{:T(128)} %constant.47.clone.1), kind=kCustom, calls=%fused_computation.147 | custom fusion | bytes 1032 | tf_op jit(solution)/shard_map/scatter | solution.py:66
  40.2 1.2 gather_fusion
  41.4 0.2 fusion
  41.5 0.1 pad_maximum_fusion
  41.7 26.0 %all_to_all.10.r_hbm.r_ref = bf16[8,96,1024]{2,1,0:T(8,128)(2,1)} all-to-all(bf16[8,96,1024]{2,1,0:T(8,128)(2,1)S(1)} %pad_maximum_fusion), channel_id=1, replica_groups=mesh['section'=4,'dp'=16,'expert'=8] {'expert'}, dimensions={0} | all-to-all | bytes 3145728 | tf_op jit(solution)/shard_map/all_to_all | solution.py:333
  67.6 22.2 %all-gather.2.cloned.1.call-done = bf16[1536,1024]{1,0:T(8,128)(2,1)} async-done(((bf16[96,1024]{1,0:T(8,128)(2,1)}), bf16[1536,1024]{1,0:T(8,128)(2,1)}) %all-gather.2.cloned.1.call-update) | async-done | bytes 3145744 | tf_op jit(solution)/shard_map/all_gather | solution.py:311
  89.8 4.9 %expert_backward.1 = (bf16[16,96,1024]{2,1,0:T(8,128)(2,1)}, bf16[256,1024]{1,0:T(8,128)(2,1)}) custom-call(bf16[16,96,1024]{2,1,0:T(8,128)(2,1)} %bitcast.136, bf16[8,96,1024]{2,1,0:T(8,128)(2,1)} %all_to_all.10.r_hbm.r_ref), custom_call_target="tpu_custom_call" | custom-call | flops 1610612736 | bytes 8388608 | tf_op jit(solution)/shard_map/expert_backward/pallas_call | solution.py:229
  94.8 0.4 fusion.24
  95.2 0.4 fusion.32
  95.6 5.1 %expert_forward.1 = bf16[8,64,1024]{2,1,0:T(8,128)(2,1)} custom-call(bf16[16,96,1024]{2,1,0:T(8,128)(2,1)} %bitcast.137, bf16[8,96,1024]{2,1,0:T(8,128)(2,1)} %all_to_all.10.r_hbm.r_ref, bf16[256,1024]{1,0:T(8,128)(2,1)} %get-tuple-element.30.g_ref), custom_call_target="tpu_custom_call" | custom-call | flops 1342177280 | bytes 6291456 | tf_op jit(solution)/shard_map/expert_forward/pallas_call | solution.py:262
  100.8 5.1 %all-to-all-start.1 = ((bf16[8,64,1024]{2,1,0:T(8,128)(2,1)}), bf16[8,64,1024]{2,1,0:T(8,128)(2,1)S(1)}, u32[]{:S(2)}, u32[]{:S(2)}) async-start(bf16[8,64,1024]{2,1,0:T(8,128)(2,1)} %expert_forward.1), calls=%async_computation.2 | async-start | bytes 2097152 | tf_op jit(solution)/shard_map/all_to_all | solution.py:345
  106.0 15.8 %all-to-all-done.1 = bf16[8,64,1024]{2,1,0:T(8,128)(2,1)S(1)} async-done(((bf16[8,64,1024]{2,1,0:T(8,128)(2,1)}), bf16[8,64,1024]{2,1,0:T(8,128)(2,1)S(1)}, u32[]{:S(2)}, u32[]{:S(2)}) %all-to-all-start.1) | async-done | bytes 1048608 | tf_op jit(solution)/shard_map/all_to_all | solution.py:345
  121.9 0.9 gather_fusion.10
  122.8 0.9 gather_fusion.9
  123.7 0.9 gather_fusion.8
  124.5 0.9 gather_fusion.7
  125.4 0.9 gather_fusion.6
  126.2 0.9 gather_fusion.5
  127.1 0.9 gather_fusion.4
  128.0 1.6 gather_fusion.3
  129.5 1.5 fusion.17
  131.0 2.3 %collective-permute-start.1 = (bf16[1,128,1024]{2,1,0:T(8,128)(2,1)S(1)}, bf16[1,128,1024]{2,1,0:T(8,128)(2,1)}, u32[]{:S(2)}, u32[]{:S(2)}) collective-permute-start(bf16[1,128,1024]{2,1,0:T(8,128)(2,1)S(1)} %fusion.17), channel_id=1, source_target_pairs={{0,128},{128,256},{256,384},{384,0},{1,129},{129,257},{257,385},{3... | collective-permute-start | bytes 786440 | tf_op jit(solution)/shard_map/ppermute | solution.py:23
  133.4 0.9 gather_fusion.18
  134.2 0.9 gather_fusion.17
  135.1 0.9 gather_fusion.16
  136.0 0.9 gather_fusion.15
  136.8 0.9 gather_fusion.14
  137.7 0.9 gather_fusion.13
  138.5 0.9 gather_fusion.12
  139.4 0.9 gather_fusion.11
  140.3 0.4 fusion.7
  140.7 0.2 fusion.23
  141.0 3.5 %collective-permute-start.2 = (bf16[1,128,1024]{2,1,0:T(8,128)(2,1)S(1)}, bf16[1,128,1024]{2,1,0:T(8,128)(2,1)S(1)}, u32[]{:S(2)}, u32[]{:S(2)}) collective-permute-start(bf16[1,128,1024]{2,1,0:T(8,128)(2,1)S(1)} %fusion.23), channel_id=1, source_target_pairs={{0,384},{128,0},{256,128},{384,256},{1,385},{129,1},{257,129},{385... | collective-permute-start | bytes 786440 | tf_op jit(solution)/shard_map/ppermute | solution.py:23
  144.5 7.0 %collective-permute-done.2.b_ref = bf16[1,128,1024]{2,1,0:T(8,128)(2,1)S(1)} collective-permute-done((bf16[1,128,1024]{2,1,0:T(8,128)(2,1)S(1)}, bf16[1,128,1024]{2,1,0:T(8,128)(2,1)S(1)}, u32[]{:S(2)}, u32[]{:S(2)}) %collective-permute-start.2) | collective-permute-done | bytes 262176 | tf_op jit(solution)/shard_map/ppermute | solution.py:23
  151.5 0.7 copy-done.3
  152.2 1.8 %land.1 = (bf16[1,128,1024]{2,1,0:T(8,128)(2,1)}, bf16[1,128,1024]{2,1,0:T(8,128)(2,1)}) custom-call(bf16[1,128,1024]{2,1,0:T(8,128)(2,1)} %collective-permute-done.1.a_ref, bf16[1,128,1024]{2,1,0:T(8,128)(2,1)} %copy-done.3), custom_call_target="tpu_custom_call" | custom-call | bytes 1048576 | tf_op jit(solution)/shard_map/land/pallas_call | solution.py:213
  154.1 12.6 %reduce-scatter.2.cloned.1.call-done = bf16[96,1024]{1,0:T(8,128)(2,1)} async-done(((bf16[1536,1024]{1,0:T(8,128)(2,1)}), bf16[96,1024]{1,0:T(8,128)(2,1)}) %reduce-scatter.2.cloned.1.call-update) | async-done | bytes 196624 | tf_op jit(solution)/shard_map/reduce_scatter | solution.py:336
  166.7 4.5 %collective-permute-start.3 = (bf16[96,1024]{1,0:T(8,128)(2,1)}, bf16[96,1024]{1,0:T(8,128)(2,1)S(1)}, u32[]{:S(2)}, u32[]{:S(2)}) collective-permute-start(bf16[96,1024]{1,0:T(8,128)(2,1)} %reduce-scatter.2.cloned.1.call-done), channel_id=1, source_target_pairs={{0,1},{1,0},{2,3},{3,2},{4,5},{5,4},{6,7},{7,6},{8,9},{9,8},{10,11... | collective-permute-start | bytes 589832 | tf_op jit(solution)/shard_map/ppermute | solution.py:41
  171.2 1.3 collective-permute-done.3.summed_ref
  172.5 0.8 unpack_grads.1
  (67 shorter events, 1.7 us)
Async XLA Ops:
  7.2 18.5 %copy-start.1 = (bf16[1,128,1024]{2,1,0:T(8,128)(2,1)S(1)}, bf16[1,128,1024]{2,1,0:T(8,128)(2,1)}, u32[]{:S(2)}) copy-start(bf16[1,128,1024]{2,1,0:T(8,128)(2,1)} %param.10) | copy-start | bytes 786436
  7.2 18.5 %copy-start = (bf16[1,128,1024]{2,1,0:T(8,128)(2,1)S(1)}, bf16[1,128,1024]{2,1,0:T(8,128)(2,1)}, u32[]{:S(2)}) copy-start(bf16[1,128,1024]{2,1,0:T(8,128)(2,1)} %param.11) | copy-start | bytes 786436
  7.2 82.6 %all-gather.2.cloned.1.call-start = ((), (), s32[]{:S(2)}) async-start(), calls=%async_computation.3 | async-start | bytes 3342336 | tf_op jit(solution)/shard_map/all_gather | solution.py:311
  8.9 3.5 %collective-permute-start = (bf16[96,1024]{1,0:T(8,128)(2,1)}, bf16[96,1024]{1,0:T(8,128)(2,1)S(1)}, u32[]{:S(2)}, u32[]{:S(2)}) collective-permute-start(bf16[96,1024]{1,0:T(8,128)(2,1)} %pack_weights.1), channel_id=1, source_target_pairs={{0,1},{1,0},{2,3},{3,2},{4,5},{5,4},{6,7},{7,6},{8,9},{9,8},{10,11... | collective-permute-start | bytes 589832 | tf_op jit(solution)/shard_map/ppermute | solution.py:41
  12.4 0.7 copy-start.4
  13.1 153.6 %reduce-scatter.2.cloned.1.call-start = ((), (), s32[]{:S(2)}) async-start(), calls=%async_computation.4 | async-start | bytes 3342336 | tf_op jit(solution)/shard_map/reduce_scatter | solution.py:336
  89.8 5.0 %copy-start.5 = (f32[1,128,8]{1,2,0:T(8,128)S(1)}, f32[1,128,8]{1,2,0:T(8,128)}, u32[]{:S(2)}) copy-start(f32[1,128,8]{1,2,0:T(8,128)} %param.14) | copy-start | bytes 12292
  100.8 21.0 %all-to-all-start.1 = ((bf16[8,64,1024]{2,1,0:T(8,128)(2,1)}), bf16[8,64,1024]{2,1,0:T(8,128)(2,1)S(1)}, u32[]{:S(2)}, u32[]{:S(2)}) async-start(bf16[8,64,1024]{2,1,0:T(8,128)(2,1)} %expert_forward.1), calls=%async_computation.2 | async-start | bytes 2097152 | tf_op jit(solution)/shard_map/all_to_all | solution.py:345
  131.0 13.5 %collective-permute-start.1 = (bf16[1,128,1024]{2,1,0:T(8,128)(2,1)S(1)}, bf16[1,128,1024]{2,1,0:T(8,128)(2,1)}, u32[]{:S(2)}, u32[]{:S(2)}) collective-permute-start(bf16[1,128,1024]{2,1,0:T(8,128)(2,1)S(1)} %fusion.17), channel_id=1, source_target_pairs={{0,128},{128,256},{256,384},{384,0},{1,129},{129,257},{257,385},{3... | collective-permute-start | bytes 786440 | tf_op jit(solution)/shard_map/ppermute | solution.py:23
  139.4 1.3 copy-start.2
  141.0 10.6 %collective-permute-start.2 = (bf16[1,128,1024]{2,1,0:T(8,128)(2,1)S(1)}, bf16[1,128,1024]{2,1,0:T(8,128)(2,1)S(1)}, u32[]{:S(2)}, u32[]{:S(2)}) collective-permute-start(bf16[1,128,1024]{2,1,0:T(8,128)(2,1)S(1)} %fusion.23), channel_id=1, source_target_pairs={{0,384},{128,0},{256,128},{384,256},{1,385},{129,1},{257,129},{385... | collective-permute-start | bytes 786440 | tf_op jit(solution)/shard_map/ppermute | solution.py:23
  151.5 0.7 copy-start.3
  166.7 5.8 %collective-permute-start.3 = (bf16[96,1024]{1,0:T(8,128)(2,1)}, bf16[96,1024]{1,0:T(8,128)(2,1)S(1)}, u32[]{:S(2)}, u32[]{:S(2)}) collective-permute-start(bf16[96,1024]{1,0:T(8,128)(2,1)} %reduce-scatter.2.cloned.1.call-done), channel_id=1, source_target_pairs={{0,1},{1,0},{2,3},{3,2},{4,5},{5,4},{6,7},{7,6},{8,9},{9,8},{10,11... | collective-permute-start | bytes 589832 | tf_op jit(solution)/shard_map/ppermute | solution.py:41
Sparse Core Ops, SparseCore 0:
  13.2 76.5 all-gather.1
  94.9 71.8 reduce-scatter.1
